TPU v7x, 512 devices: a whole 4x4x16 slice. The times are simulated.
512 devices in a mesh: ha: 128 (over z, x, core), ta: 4 (over y).
Axes of the slice: x: 4, y: 4, z: 16, core: 2. Of those that a mesh axis runs over, the one named last changes fastest.
Arguments:
- ref_feats: bfloat16 [32, 128, 512], P(None, None, 'ta'), may hold values from -16 to 16
- crops: bfloat16 [128, 32, 160, 512], P('ha', None, None, 'ta'), may hold values from -6 to 6
- owner: int32 [2], replicated, may hold values from 0 to 127
- offsets: int32 [2, 256], replicated, may hold values from 0 to 28
- bands: int32 [2, 256], replicated, may hold values from 1 to 4
- taps: float32 [2, 256, 4], replicated, may hold values from 0.2 to 1
- filt: float32 [8, 3, 3], replicated, may hold values from -2.8 to 5.3
Outputs:
- depth: float32 [128, 512], P('ha', 'ta')
All inputs are finite; a program needn't handle non-finite values.
Results may differ from a plain program's by a relative error of at most 0.0067.
Values may be sent and summed in bfloat16 or wider, within the bound.
No kernel may reach another device: no remote copies, remote signals or barrier semaphores. Data moves between devices by JAX's collectives and lax.ppermute only.
A program may use at most 64 MiB of HBM per device.

v0:
```python
import jax
import jax.numpy as jnp
from jax import lax
from jax.sharding import PartitionSpec as P

G = 8


def extended(cells, sides, width):
    for axis, dim in sides:
        count = lax.axis_size(axis)
        ends = count - 1
        head = lax.slice_in_dim(cells, 0, width, axis=dim)
        tail = lax.slice_in_dim(cells, cells.shape[dim] - width, cells.shape[dim], axis=dim)
        cells = jnp.concatenate(
            [
                lax.ppermute(tail, axis, [(i, (i + 1) % count) for i in range(ends)]),
                cells,
                lax.ppermute(head, axis, [((i + 1) % count, i) for i in range(ends)]),
            ],
            axis=dim,
        )
    return cells


def broadcast(value, axis, source):
    kept = jnp.where(lax.axis_index(axis) == source, value, 0).astype(value.dtype)
    return lax.psum(kept, axis)


def plane_corr(ref_feats, crop, shift_rows, band_width, tap_row):
    active = jnp.arange(tap_row.shape[0]) < band_width
    weights = jnp.where(active, tap_row, 0.0)
    weights = weights / jnp.sum(weights)
    channels, rows, cols = ref_feats.shape
    warped = jnp.zeros((channels, rows, cols), jnp.float32)
    for tap_index in range(tap_row.shape[0]):
        window = lax.dynamic_slice_in_dim(crop, shift_rows + tap_index, rows, 1)
        warped = warped + weights[tap_index] * window.astype(jnp.float32)
    product = ref_feats.astype(jnp.float32) * warped
    grouped = product.reshape(G, channels // G, rows, cols)
    return jnp.sum(grouped, axis=1) / (channels // G)


def plane_cost(padded, filt, count, cols):
    cost = jnp.zeros((count, padded.shape[2], cols), jnp.float32)
    for plane_lag in range(3):
        for column_lag in range(3):
            slab = padded[
                plane_lag : plane_lag + count, :, :, column_lag : column_lag + cols
            ].astype(jnp.float32)
            cost = cost + jnp.sum(
                slab * filt[:, plane_lag, column_lag][None, :, None, None], axis=1
            )
    return cost


def column_edges(volume):
    return extended(volume, (("ta", 3),), 1)


def body(ref_feats, crops, owner, offsets, bands, taps, filt):
    planes_all = offsets.shape[1]
    planes_here = planes_all // lax.axis_size("ha")
    first = lax.axis_index("ha") * planes_here
    rows = ref_feats.shape[1]
    cols = ref_feats.shape[2]
    views = owner.shape[0]
    corr_planes = jax.vmap(plane_corr, in_axes=(None, None, 0, 0, 0))
    total_shape = (planes_here, G, rows, cols)
    total = jnp.zeros(total_shape, jnp.float32)
    for view in range(views):
        crop = broadcast(crops[0], "ha", owner[view])
        shifts = lax.dynamic_slice_in_dim(offsets[view], first, planes_here)
        widths = lax.dynamic_slice_in_dim(bands[view], first, planes_here)
        tap_rows = lax.dynamic_slice_in_dim(taps[view], first, planes_here, 0)
        total = total + corr_planes(ref_feats, crop, shifts, widths, tap_rows)
    volume = (total / views).astype(jnp.bfloat16)
    row_volume = lax.all_to_all(volume, "ha", split_axis=2, concat_axis=0, tiled=True)
    edged = column_edges(row_volume)
    edged = jnp.pad(edged, ((1, 1), (0, 0), (0, 0), (0, 0)))
    cost = plane_cost(edged, filt, planes_all, cols)
    probs = jax.nn.softmax(cost, axis=0)
    heights = jnp.arange(planes_all).astype(jnp.float32) / (planes_all - 1)
    depth = jnp.sum(probs * heights[:, None, None], axis=0)
    return depth


def solution(mesh):
    placed = (P(None, None, "ta"), P("ha", None, None, "ta"), P(), P(), P(), P(), P())
    return jax.shard_map(body, mesh=mesh, in_specs=placed, out_specs=P("ha", "ta"), check_vma=False)
```

profile of v0, /device:TPU:32, one launch (start us, length us, event | category | flops | bytes accessed | tf_op | source)
XLA Modules:
  0.0 481.7 jit_solution(12069070403212359317)
XLA Ops:
  6.5 0.0 all-reduce.4.cloned.1.call-start
  6.5 1.4 fusion.46
  9.3 3.3 select_bitcast_fusion.1
  12.6 0.0 copy-start.4
  12.6 0.0 copy-start.6
  12.6 0.0 copy-start.7
  12.6 0.0 copy-start.3
  12.6 0.0 all-reduce.4.cloned.1.call-update
  12.6 0.7 copy-done.4
  13.3 0.1 constant_dynamic-slice_fusion.1
  13.4 0.1 copy.34
  13.5 0.0 copy-done.6
  13.5 0.1 copy.32
  13.6 0.0 copy-done.7
  13.6 0.3 copy-done.3
  13.9 2.2 copy.31
  16.0 0.1 fusion.22
  16.1 0.2 fusion.21
  16.3 0.1 fusion.28
  16.4 0.1 fusion.20
  16.4 0.2 slice_reduce_fusion.3
  16.7 0.2 fusion.19
  16.8 0.1 fusion.18
  16.9 0.2 slice_reduce_fusion.7
  17.2 350.5 %all-reduce.4.cloned.1.call-done = (bf16[32,160,128]{2,0,1:T(8,128)(2,1)}, bf16[32,160,128]{2,0,1:T(8,128)(2,1)}) async-done(((bf16[32,160,128]{2,0,1:T(8,128)(2,1)}, bf16[32,160,128]{2,0,1:T(8,128)(2,1)}), (bf16[32,160,128]{2,0,1:T(8,128)(2,1)}, bf16[32,160,128]{2,0,1:T(8,128)(2,1)})) %all-reduce.4.cloned.1.call-update) | async-done | bytes 2621456 | tf_op jit(solution)/shard_map/psum | solution.py:28
  367.7 0.0 copy-start.1
  367.7 3.6 gather_fusion.1
  371.2 0.0 copy-done.1
  371.2 2.1 gather_fusion.2
  373.4 0.0 copy-start
  373.4 2.1 gather_fusion.3
  375.5 0.0 copy-done
  375.5 2.2 gather_fusion.5
  377.7 2.1 gather_fusion.6
  379.8 2.2 gather_fusion.7
  382.0 2.2 gather_fusion
  384.2 0.0 copy-start.2
  384.2 2.1 gather_fusion.4
  386.3 0.0 copy-done.2
  386.3 14.6 %fusion.2 = (f32[2,8,128,128]{3,1,2,0:T(8,128)S(1)}, f32[2,8,128,128]{3,1,2,0:T(8,128)S(1)}) fusion(bf16[2,8,4,128,128]{4,2,1,3,0:T(4,128)(2,1)} %bitcast.124, bf16[2,8,4,128,128]{4,2,1,3,0:T(4,128)(2,1)} %bitcast.123, bf16[2,8,4,128,128]{4,2,1,3,0:T(4,128)(2,1)} %bitcast.122, bf16[2,8,4,128,128]{4,2,1,3,0:T(4,128)(2,1)} %bitcast.126, ...), kind=kLoop, calls=%fused_computation.11 | loop fusion | flops 26738688 | bytes 20971584 | tf_op jit(solution)/shard_map/vmap()/reduce_sum | solution.py:42
  401.0 0.0 copy-start.5
  401.0 0.1 multiply_convert_fusion
  401.1 0.9 copy.36
  402.0 15.4 %all-to-all-start = ((bf16[2,8,128,128]{3,1,0,2:T(8,128)(2,1)}), bf16[2,8,128,128]{3,1,0,2:T(8,128)(2,1)S(1)}, u32[]{:S(2)}, u32[]{:S(2)}) async-start(bf16[2,8,128,128]{3,1,0,2:T(8,128)(2,1)} %copy.36), calls=%async_computation | async-start | bytes 1048576 | tf_op jit(solution)/shard_map/all_to_all | solution.py:79
  417.4 0.0 copy-done.5
  417.4 33.0 %all-to-all-done = bf16[2,8,128,128]{3,1,0,2:T(8,128)(2,1)S(1)} async-done(((bf16[2,8,128,128]{3,1,0,2:T(8,128)(2,1)}), bf16[2,8,128,128]{3,1,0,2:T(8,128)(2,1)S(1)}, u32[]{:S(2)}, u32[]{:S(2)}) %all-to-all-start) | async-done | bytes 524320 | tf_op jit(solution)/shard_map/all_to_all | solution.py:79
  450.4 0.2 fusion.42
  450.6 3.4 collective-permute-start
  454.1 1.5 collective-permute-start.1
  455.6 0.6 multiply_reduce_fusion.4
  456.1 9.9 %collective-permute-done = bf16[256,8,1,1]{3,1,0,2:T(8,128)(2,1)S(1)} collective-permute-done((bf16[256,8,1,1]{3,1,0,2:T(8,128)(2,1)S(1)}, bf16[256,8,1,1]{3,1,0,2:T(8,128)(2,1)S(1)}, u32[]{:S(2)}, u32[]{:S(2)}) %collective-permute-start) | collective-permute-done | bytes 4128 | tf_op jit(solution)/shard_map/ppermute | solution.py:17
  466.1 4.2 collective-permute-done.1
  470.2 0.7 fusion.15
  470.9 2.1 multiply_reduce_fusion.7
  473.0 1.1 multiply_reduce_fusion.5
  474.1 0.1 add_reduce_fusion
  474.2 0.1 fusion.38
  474.3 0.6 multiply_reduce_fusion.9
  (7 shorter events, 0.0 us)
Async XLA Ops:
  6.5 361.1 %all-reduce.4.cloned.1.call-start = ((), (), s32[]{:S(2)}) async-start(), calls=%async_computation.1 | async-start | bytes 5242880 | tf_op jit(solution)/shard_map/psum | solution.py:28
  12.6 0.7 copy-start.4
  12.6 0.9 copy-start.6
  12.6 1.0 copy-start.7
  12.6 1.3 copy-start.3
  367.7 3.6 copy-start.1
  373.4 2.1 copy-start
  384.2 2.2 copy-start.2
  401.0 16.4 %copy-start.5 = (f32[8,3,3]{0,2,1:T(4,128)S(1)}, f32[8,3,3]{0,2,1:T(4,128)}, u32[]{:S(2)}) copy-start(f32[8,3,3]{0,2,1:T(4,128)} %param.13) | copy-start | bytes 868
  402.0 48.4 %all-to-all-start = ((bf16[2,8,128,128]{3,1,0,2:T(8,128)(2,1)}), bf16[2,8,128,128]{3,1,0,2:T(8,128)(2,1)S(1)}, u32[]{:S(2)}, u32[]{:S(2)}) async-start(bf16[2,8,128,128]{3,1,0,2:T(8,128)(2,1)} %copy.36), calls=%async_computation | async-start | bytes 1048576 | tf_op jit(solution)/shard_map/all_to_all | solution.py:79
  450.6 15.4 %collective-permute-start = (bf16[256,8,1,1]{3,1,0,2:T(8,128)(2,1)S(1)}, bf16[256,8,1,1]{3,1,0,2:T(8,128)(2,1)S(1)}, u32[]{:S(2)}, u32[]{:S(2)}) collective-permute-start(bf16[256,8,1,1]{3,1,0,2:T(8,128)(2,1)S(1)} %get-tuple-element.35), channel_id=1, source_target_pairs={{0,1},{1,2},{2,3},{4,5},{5,6},{6,7},{8,9},{9,10},{10,11},{12,13},{... | collective-permute-start | bytes 12296 | tf_op jit(solution)/shard_map/ppermute | solution.py:17
  454.1 16.2 %collective-permute-start.1 = (bf16[256,8,1,1]{3,1,0,2:T(8,128)(2,1)S(1)}, bf16[256,8,1,1]{3,1,0,2:T(8,128)(2,1)S(1)}, u32[]{:S(2)}, u32[]{:S(2)}) collective-permute-start(bf16[256,8,1,1]{3,1,0,2:T(8,128)(2,1)S(1)} %get-tuple-element.36), channel_id=1, source_target_pairs={{1,0},{2,1},{3,2},{5,4},{6,5},{7,6},{9,8},{10,9},{11,10},{13,12},{... | collective-permute-start | bytes 12296 | tf_op jit(solution)/shard_map/ppermute | solution.py:19
Sparse Core Ops, SparseCore 0:
  12.7 354.8 all-reduce.3
where the time goes:
time: 482 us
  waiting for transfers between devices  398 us (83%)
  local copies, waits for them, and re-layouts  25.1 us (5%)
  other arithmetic  23.9 us (5%)
  starting transfers between devices  20.3 us (4%)
  between operations  14.9 us (3%)
    psum x1, waiting for transfers between devices, broadcast(): return lax.psum(kept, axis)  350 us
    all_to_all x1, waiting for transfers between devices, body(): lax.all_to_all(volume, 'ha', split_axis=2, concat_axis=0, tiled=True)  33 us
    gather x8, local copies, waits for them, and re-layouts, plane_corr(): window = lax.dynamic_slice_in_dim(crop, shift_rows + tap_index, rows, 1)  18.6 us
    all_to_all x1, starting transfers between devices, body(): lax.all_to_all(volume, 'ha', split_axis=2, concat_axis=0, tiled=True)  15.4 us
    reduce_sum x1, other arithmetic, plane_corr(): return jnp.sum(grouped, axis=1) / (channels // G)  14.6 us
    ppermute x1, waiting for transfers between devices, extended(): lax.ppermute(tail, axis, [(i, (i + 1) % count) for i in range(ends)])  9.94 us
  transfers between devices with their start and end apart: 4, of which 4 were waited for; matrix products, arithmetic and copies ran while one was open for 1% of the time, Pallas kernels for 0%

commit v1 on v0

v1 whole, which is shorter than its diff:
```python
import jax
import jax.numpy as jnp
from jax import lax
from jax.experimental import pallas as pl
from jax.experimental.pallas import tpu as pltpu
from jax.sharding import Mesh, PartitionSpec as P

G = 8
CG = 4
D = 256
ZH, ZL, NX, NC = 4, 4, 4, 2
SPAN = 32


def arrange(meta, first, second, out, rows):
    for view, source in enumerate((first, second)):
        for chan in range(CG):
            rows[...] = source[0, chan].astype(jnp.float32)
            for block in range(ZH):
                for phase in range(ZL):
                    picked = rows[pl.ds(SPAN * block + phase, 16, stride=ZL), :]
                    out[block * ZL + phase, view, chan] = picked.astype(jnp.bfloat16)


def arrange_call(meta, arrived):
    spec = pl.BlockSpec((1, CG, 160, 128), lambda i, m: (m[0], 0, 0, 0))
    spec_b = pl.BlockSpec((1, CG, 160, 128), lambda i, m: (m[1], 0, 0, 0))
    return pl.pallas_call(
        arrange,
        grid_spec=pltpu.PrefetchScalarGridSpec(
            num_scalar_prefetch=1,
            grid=(1,),
            in_specs=[spec, spec_b],
            out_specs=pl.BlockSpec((16, 2, CG, 16, 128), lambda i, m: (0, 0, 0, 0, 0)),
            scratch_shapes=[pltpu.VMEM((160, 128), jnp.float32)],
        ),
        out_shape=jax.ShapeDtypeStruct((16, 2, CG, 16, 128), jnp.bfloat16),
        name="arrange",
    )(meta, arrived, arrived)


def products(meta, first, second, ref, out, rows, refs):
    phase = meta[5]
    for view, source in enumerate((first, second)):
        for chan in range(CG):
            rows[view, chan] = source[0, 0, chan].astype(jnp.float32)
    for chan in range(CG):
        refs[chan] = ref[chan].astype(jnp.float32)
    for row in range(SPAN):
        start = row // ZL + jnp.where(row % ZL > phase, 1, 0)
        for view in range(2):
            total = jnp.zeros((8, 128), jnp.float32)
            for chan in range(CG):
                line = refs[chan, row : row + 1, :]
                total = total + line * rows[view, chan, pl.ds(start, 8), :]
            out[row, view] = total


def products_call(meta, arrived, ref):
    def spec(view):
        return pl.BlockSpec((1, 1, CG, 16, 128), lambda i, m: (m[2 + view], view, 0, 0, 0))

    return pl.pallas_call(
        products,
        grid_spec=pltpu.PrefetchScalarGridSpec(
            num_scalar_prefetch=1,
            grid=(1,),
            in_specs=[
                spec(0),
                spec(1),
                pl.BlockSpec((CG, SPAN, 128), lambda i, m: (m[6], m[4], 0)),
            ],
            out_specs=pl.BlockSpec((SPAN, 2, 8, 128), lambda i, m: (0, 0, 0, 0)),
            scratch_shapes=[
                pltpu.VMEM((2, CG, 16, 128), jnp.float32),
                pltpu.VMEM((CG, SPAN, 128), jnp.float32),
            ],
        ),
        out_shape=jax.ShapeDtypeStruct((SPAN, 2, 8, 128), jnp.float32),
        name="products",
    )(meta, arrived, arrived, ref)


def weigh(meta, offsets, bands, taps, out):
    sub = lax.broadcasted_iota(jnp.int32, (128, D), 0)
    packed = jnp.zeros((128, D), jnp.float32)
    for view in range(2):
        packed = jnp.where(sub == view, offsets[view : view + 1, :].astype(jnp.float32), packed)
        packed = jnp.where(sub == 2 + view, bands[view : view + 1, :].astype(jnp.float32), packed)
    packed = packed.T
    lane = lax.broadcasted_iota(jnp.int32, (D, 128), 1)
    shift = jnp.bitwise_and(lane // 16 + 4 - jnp.bitwise_and(meta[6], 3), 3)
    reach = (shift + 4 * jnp.bitwise_and(lane, 7)).astype(jnp.float32)
    side = jnp.bitwise_and(lane // 8, 1)
    total = jnp.zeros((D, 128), jnp.float32)
    for view in range(2):
        offset = packed[:, view : view + 1]
        band = packed[:, 2 + view : 3 + view]
        kept = [jnp.where(band > k, taps[view, :, k : k + 1], 0.0) for k in range(4)]
        whole = kept[0] + kept[1] + kept[2] + kept[3]
        lag = jnp.where(side == view, reach, -1.0) - offset
        for k in range(4):
            total = jnp.where(lag == k, kept[k] / whole, total)
    high = total.astype(jnp.bfloat16)
    out[:, :128] = high
    out[:, 128:] = (total - high.astype(jnp.float32)).astype(jnp.bfloat16)


def weigh_call(meta, offsets, bands, taps):
    return pl.pallas_call(
        weigh,
        grid_spec=pltpu.PrefetchScalarGridSpec(
            num_scalar_prefetch=1,
            grid=(1,),
            in_specs=[
                pl.BlockSpec((2, D), lambda i, m: (0, 0)),
                pl.BlockSpec((2, D), lambda i, m: (0, 0)),
                pl.BlockSpec((2, D, 4), lambda i, m: (0, 0, 0)),
            ],
            out_specs=pl.BlockSpec((D, 256), lambda i, m: (0, 0)),
        ),
        out_shape=jax.ShapeDtypeStruct((D, 256), jnp.bfloat16),
        name="weigh",
    )(meta, offsets, bands, taps)


def filtered(filt, weights, pieces, cost, right, left, stack, volume, sums):
    for group in range(G):
        lanes = slice(128 * group, 128 * group + 128)
        for block in range(ZL):
            piece = pieces[block * G + group].reshape(16, 128)
            high = piece.astype(jnp.bfloat16)
            low = (piece - high.astype(jnp.float32)).astype(jnp.bfloat16)
            for copy in range(2):
                at = 128 * copy + 16 * block
                stack[at : at + 16, lanes] = high
                stack[at + 64 : at + 80, lanes] = low
    volume[...] = jnp.dot(weights[...], stack[...], preferred_element_type=jnp.float32)
    zero = jnp.zeros((8, 128), jnp.float32)
    for i in range(3):
        for j in range(3):
            sums[i, j, 0:8, :] = zero
            sums[i, j, D + 8 : D + 16, :] = zero
    step = 32

    def strip(index, carry):
        at = pl.multiple_of(index * step, step)
        totals = [[jnp.zeros((step, 128), jnp.float32) for _ in range(3)] for _ in range(3)]
        for group in range(G):
            part = volume[pl.ds(at, step), 128 * group : 128 * group + 128] * 0.125
            part = part.astype(jnp.bfloat16).astype(jnp.float32)
            for i in range(3):
                for j in range(3):
                    totals[i][j] = totals[i][j] + filt[group * 9 + i * 3 + j] * part
        for i in range(3):
            for j in range(3):
                sums[i, j, pl.ds(at + 8, step), :] = totals[i][j]
        return carry

    lax.fori_loop(0, D // step, strip, 0)
    lane = lax.broadcasted_iota(jnp.int32, (D, 128), 1)
    column = [sums[0, j, 7 : D + 7, :] + sums[1, j, 8 : D + 8, :] + sums[2, j, 9 : D + 9, :] for j in range(3)]
    before = pltpu.roll(column[0], 1, 1)
    after = pltpu.roll(column[2], 127, 1)
    cost[...] = column[1] + jnp.where(lane == 0, 0.0, before) + jnp.where(lane == 127, 0.0, after)
    edges = jnp.where(lane == 0, before, after).T
    right[...] = edges[0:1, :]
    left[...] = edges[127:128, :]


def filtered_call(filt, weights, pieces):
    edge = jax.ShapeDtypeStruct((1, D), jnp.float32)
    return pl.pallas_call(
        filtered,
        in_specs=[
            pl.BlockSpec(memory_space=pltpu.SMEM),
            pl.BlockSpec(memory_space=pltpu.VMEM),
            pl.BlockSpec(memory_space=pltpu.VMEM),
        ],
        out_shape=[jax.ShapeDtypeStruct((D, 128), jnp.float32), edge, edge],
        scratch_shapes=[
            pltpu.VMEM((256, 1024), jnp.bfloat16),
            pltpu.VMEM((D, 1024), jnp.float32),
            pltpu.VMEM((3, 3, D + 16, 128), jnp.float32),
        ],
        name="filtered",
    )(filt, weights, pieces)


def expected(cost, from_left, from_right, out):
    sub = lax.broadcasted_iota(jnp.int32, (128, D), 0)
    edges = jnp.where(sub == 0, from_left[...], jnp.where(sub == 127, from_right[...], 0.0)).T
    whole = cost[...] + edges
    top = jnp.max(whole, axis=0, keepdims=True)
    grown = jnp.exp(whole - top)
    heights = lax.broadcasted_iota(jnp.int32, (D, 128), 0).astype(jnp.float32) * (1.0 / (D - 1))
    out[...] = jnp.sum(grown * heights, axis=0, keepdims=True) / jnp.sum(grown, axis=0, keepdims=True)


def expected_call(cost, from_left, from_right):
    return pl.pallas_call(
        expected,
        out_shape=jax.ShapeDtypeStruct((1, 128), jnp.float32),
        name="expected",
    )(cost, from_left, from_right)


def body(ref_feats, crops, owner, offsets, bands, taps, filt):
    block = lax.axis_index("zh")
    phase = lax.axis_index("zl")
    group = lax.axis_index("x") * NC + lax.axis_index("c")
    near = owner % G
    far = owner // G
    meta = jnp.stack([near[0], near[1], far[0], far[1], block, phase, group]).astype(jnp.int32)
    arrived = lax.all_to_all(crops[0], ("x", "c"), 0, 0, tiled=True)
    weights = weigh_call(meta, offsets, bands, taps)
    windows = arrange_call(meta, arrived.reshape(G, CG, 160, 128))
    windows = lax.all_to_all(windows, ("zh", "zl"), 0, 0, tiled=True)
    pieces = products_call(meta, windows, ref_feats)
    pieces = lax.all_to_all(pieces, ("zl", "x", "c"), 0, 0, tiled=True)
    cost, right, left = filtered_call(filt.reshape(G * 9), weights, pieces)
    count = lax.axis_size("ta")
    from_left = lax.ppermute(right, "ta", [(i, i + 1) for i in range(count - 1)])
    from_right = lax.ppermute(left, "ta", [(i + 1, i) for i in range(count - 1)])
    return expected_call(cost, from_left, from_right)


def solution(mesh):
    rows = ("zh", "zl", "x", "c")
    inner = Mesh(mesh.devices.reshape(ZH, ZL, NX, NC, mesh.shape["ta"]), rows + ("ta",))
    placed = (P(None, None, "ta"), P(rows, None, None, "ta"), P(), P(), P(), P(), P())
    return jax.shard_map(body, mesh=inner, in_specs=placed, out_specs=P(rows, "ta"), check_vma=False)
```

time: 482 us -> 105 us (0.22)
  the two profiles are of different devices: /device:TPU:32 before, /device:TPU:8 now
where the time goes in v1:
time: 105 us
  blocking collectives  44.1 us (42%)
  waiting for transfers between devices  27.9 us (27%)
  starting transfers between devices  15.5 us (15%)
  Pallas kernels  12.6 us (12%)
  local copies, waits for them, and re-layouts  4.54 us (4%)
    all_to_all x1, blocking collectives, body(): windows = lax.all_to_all(windows, ('zh', 'zl'), 0, 0, tiled=True)  44.1 us
    all_to_all x1, waiting for transfers between devices, body(): arrived = lax.all_to_all(crops[0], ('x', 'c'), 0, 0, tiled=True)  18.2 us
    all_to_all x1, waiting for transfers between devices, body(): pieces = lax.all_to_all(pieces, ('zl', 'x', 'c'), 0, 0, tiled=True)  6.47 us
    all_to_all x1, starting transfers between devices, body(): pieces = lax.all_to_all(pieces, ('zl', 'x', 'c'), 0, 0, tiled=True)  5.26 us
    all_to_all x1, starting transfers between devices, body(): arrived = lax.all_to_all(crops[0], ('x', 'c'), 0, 0, tiled=True)  4.43 us
    ppermute x1, starting transfers between devices, body(): lax.ppermute(right, 'ta', [(i, i + 1) for i in range(count - 1)])  3.47 us
    unnamed x16, local copies, waits for them, and re-layouts  3.32 us
    ppermute x1, waiting for transfers between devices, body(): lax.ppermute(left, 'ta', [(i + 1, i) for i in range(count - 1)])  3.29 us
  transfers between devices with their start and end apart: 4, of which 3 were waited for; matrix products, arithmetic and copies ran while one was open for 2% of the time, Pallas kernels for 3%

profile of v1, /device:TPU:8, one launch (start us, length us, event | category | flops | bytes accessed | tf_op | source)
XLA Modules:
  0.0 104.8 jit_solution(14241247110757610283)
XLA Ops:
  0.0 0.0 copy-start.6
  0.0 4.4 %all-to-all-start = ((bf16[32,160,128]{2,1,0:T(8,128)(2,1)}), bf16[32,160,128]{2,1,0:T(8,128)(2,1)S(1)}, u32[]{:S(2)}, u32[]{:S(2)}) async-start(bf16[32,160,128]{2,1,0:T(8,128)(2,1)} %bitcast.7), calls=%async_computation | async-start | bytes 2621440 | tf_op jit(solution)/shard_map/all_to_all | solution.py:215
  4.4 0.0 copy-done.6
  4.5 0.6 stack.15.meta
  5.1 18.2 %all-to-all-done = bf16[32,160,128]{2,1,0:T(8,128)(2,1)S(1)} async-done(((bf16[32,160,128]{2,1,0:T(8,128)(2,1)}), bf16[32,160,128]{2,1,0:T(8,128)(2,1)S(1)}, u32[]{:S(2)}, u32[]{:S(2)}) %all-to-all-start) | async-done | bytes 1310752 | tf_op jit(solution)/shard_map/all_to_all | solution.py:215
  23.2 0.0 copy-start
  23.2 1.1 %copy-done = bf16[32,160,128]{2,1,0:T(8,128)(2,1)} copy-done((bf16[32,160,128]{2,1,0:T(8,128)(2,1)}, bf16[32,160,128]{2,1,0:T(8,128)(2,1)S(1)}, u32[]{:S(2)}) %copy-start) | copy-done | bytes 1310744
  24.3 2.6 %arrange.1 = bf16[16,2,4,16,128]{4,3,2,1,0:T(8,128)(2,1)} custom-call(s32[7]{0:T(128)} %stack.15.meta, bf16[8,4,160,128]{3,2,1,0:T(8,128)(2,1)} %bitcast.5, bf16[8,4,160,128]{3,2,1,0:T(8,128)(2,1)} %bitcast.6), custom_call_target="tpu_custom_call" | custom-call | tf_op jit(solution)/shard_map/arrange/pallas_call | solution.py:28
  26.9 44.1 %all_to_all.15.first.second = bf16[16,2,4,16,128]{4,3,2,1,0:T(8,128)(2,1)} all-to-all(bf16[16,2,4,16,128]{4,3,2,1,0:T(8,128)(2,1)} %arrange.1), channel_id=1, replica_groups=mesh['zh'=4,'zl'=4,'x'=4,'c'=2,'ta'=4] {'zh','zl'}, dimensions={0} | all-to-all | bytes 1048576 | tf_op jit(solution)/shard_map/all_to_all | solution.py:218
  71.0 0.0 copy-start.3
  71.0 0.0 copy-start.2
  71.0 2.4 %products.1 = f32[32,2,8,128]{3,2,1,0:T(8,128)} custom-call(s32[7]{0:T(128)} %stack.15.meta, bf16[16,2,4,16,128]{4,3,2,1,0:T(8,128)(2,1)} %all_to_all.15.first.second, bf16[16,2,4,16,128]{4,3,2,1,0:T(8,128)(2,1)} %all_to_all.15.first.second, bf16[32,128,128]{2,1,0:T(8,128)(2,1)} %ref.1), custom_call_target="tpu_custom_call" | custom-call | tf_op jit(solution)/shard_map/products/pallas_call | solution.py:63
  73.4 5.3 %all-to-all-start.2 = ((f32[32,2,8,128]{3,2,1,0:T(8,128)}), f32[32,2,8,128]{3,2,1,0:T(8,128)S(1)}, u32[]{:S(2)}, u32[]{:S(2)}) async-start(f32[32,2,8,128]{3,2,1,0:T(8,128)} %products.1), calls=%async_computation.2 | async-start | bytes 524288 | tf_op jit(solution)/shard_map/all_to_all | solution.py:220
  78.7 0.0 copy-done.3
  78.7 0.1 copy.10
  78.8 0.6 reshape.6.filt
  79.4 0.0 copy-done.2
  79.4 0.9 copy.11.taps
  80.3 3.0 %weigh.1.weights = bf16[256,256]{1,0:T(8,128)(2,1)} custom-call(s32[7]{0:T(128)} %stack.15.meta, s32[2,256]{1,0:T(2,128)} %offsets.1, s32[2,256]{1,0:T(2,128)} %bands.1, f32[2,256,4]{2,1,0:T(8,128)} %copy.11.taps), custom_call_target="tpu_custom_call" | custom-call | tf_op jit(solution)/shard_map/weigh/pallas_call | solution.py:110
  83.3 6.5 %all-to-all-done.2.pieces = f32[32,2,8,128]{3,2,1,0:T(8,128)S(1)} async-done(((f32[32,2,8,128]{3,2,1,0:T(8,128)}), f32[32,2,8,128]{3,2,1,0:T(8,128)S(1)}, u32[]{:S(2)}, u32[]{:S(2)}) %all-to-all-start.2) | async-done | bytes 262176 | tf_op jit(solution)/shard_map/all_to_all | solution.py:220
  89.8 0.0 copy-start.1
  89.8 0.7 copy-done.1
  90.5 3.0 %filtered.1 = (f32[256,128]{1,0:T(8,128)}, f32[1,256]{1,0:T(1,128)}, f32[1,256]{1,0:T(1,128)}) custom-call(f32[72]{0:T(128)} %reshape.6.filt, bf16[256,256]{1,0:T(8,128)(2,1)} %weigh.1.weights, f32[32,2,8,128]{3,2,1,0:T(8,128)} %copy-done.1), custom_call_target="tpu_custom_call" | custom-call | tf_op jit(solution)/shard_map/filtered/pallas_call | solution.py:173
  93.5 3.5 %collective-permute-start = (f32[1,256]{1,0:T(1,128)}, f32[1,256]{1,0:T(1,128)S(1)}, u32[]{:S(2)}, u32[]{:S(2)}) collective-permute-start(f32[1,256]{1,0:T(1,128)} %get-tuple-element.9), channel_id=1, source_target_pairs={{0,1},{1,2},{2,3},{4,5},{5,6},{6,7},{8,9},{9,10},{10,11},{12,13},{... | collective-permute-start | bytes 3080 | tf_op jit(solution)/shard_map/ppermute | solution.py:223
  97.0 2.4 %collective-permute-start.1 = (f32[1,256]{1,0:T(1,128)}, f32[1,256]{1,0:T(1,128)S(1)}, u32[]{:S(2)}, u32[]{:S(2)}) collective-permute-start(f32[1,256]{1,0:T(1,128)} %get-tuple-element.10), channel_id=1, source_target_pairs={{1,0},{2,1},{3,2},{5,4},{6,5},{7,6},{9,8},{10,9},{11,10},{13,12},{... | collective-permute-start | bytes 3080 | tf_op jit(solution)/shard_map/ppermute | solution.py:224
  99.3 0.0 collective-permute-done.from_left
  99.3 0.0 copy-start.4
  99.3 3.3 %collective-permute-done.1.from_right = f32[1,256]{1,0:T(1,128)S(1)} collective-permute-done((f32[1,256]{1,0:T(1,128)}, f32[1,256]{1,0:T(1,128)S(1)}, u32[]{:S(2)}, u32[]{:S(2)}) %collective-permute-start.1) | collective-permute-done | bytes 1056 | tf_op jit(solution)/shard_map/ppermute | solution.py:224
  102.6 0.0 copy-start.5
  102.6 0.0 copy-done.4
  102.6 0.6 copy-done.5
  103.2 1.6 %expected.1 = f32[1,128]{1,0:T(1,128)} custom-call(f32[256,128]{1,0:T(8,128)} %get-tuple-element.8.cost, f32[1,256]{1,0:T(1,128)} %copy-done.4, f32[1,256]{1,0:T(1,128)} %copy-done.5), custom_call_target="tpu_custom_call" | custom-call | tf_op jit(solution)/shard_map/expected/pallas_call | solution.py:201
  (1 shorter events, 0.0 us)
Async XLA Ops:
  0.0 4.4 %copy-start.6 = (s32[2]{0:T(128)S(1)}, s32[2]{0:T(128)}, u32[]{:S(2)}) copy-start(s32[2]{0:T(128)} %param.9) | copy-start | bytes 28
  0.0 23.2 %all-to-all-start = ((bf16[32,160,128]{2,1,0:T(8,128)(2,1)}), bf16[32,160,128]{2,1,0:T(8,128)(2,1)S(1)}, u32[]{:S(2)}, u32[]{:S(2)}) async-start(bf16[32,160,128]{2,1,0:T(8,128)(2,1)} %bitcast.7), calls=%async_computation | async-start | bytes 2621440 | tf_op jit(solution)/shard_map/all_to_all | solution.py:215
  23.2 1.1 %copy-start = (bf16[32,160,128]{2,1,0:T(8,128)(2,1)}, bf16[32,160,128]{2,1,0:T(8,128)(2,1)S(1)}, u32[]{:S(2)}) copy-start(bf16[32,160,128]{2,1,0:T(8,128)(2,1)S(1)} %all-to-all-done) | copy-start | bytes 3932164
  71.0 7.7 %copy-start.3 = (f32[8,3,3]{0,2,1:T(4,128)S(1)}, f32[8,3,3]{0,2,1:T(4,128)}, u32[]{:S(2)}) copy-start(f32[8,3,3]{0,2,1:T(4,128)} %param.13) | copy-start | bytes 868
  71.0 8.4 %copy-start.2 = (f32[2,256,4]{1,2,0:T(4,128)S(1)}, f32[2,256,4]{1,2,0:T(4,128)}, u32[]{:S(2)}) copy-start(f32[2,256,4]{1,2,0:T(4,128)} %param.12) | copy-start | bytes 24580
  73.4 16.4 %all-to-all-start.2 = ((f32[32,2,8,128]{3,2,1,0:T(8,128)}), f32[32,2,8,128]{3,2,1,0:T(8,128)S(1)}, u32[]{:S(2)}, u32[]{:S(2)}) async-start(f32[32,2,8,128]{3,2,1,0:T(8,128)} %products.1), calls=%async_computation.2 | async-start | bytes 524288 | tf_op jit(solution)/shard_map/all_to_all | solution.py:220
  89.8 0.7 copy-start.1
  93.5 5.8 %collective-permute-start = (f32[1,256]{1,0:T(1,128)}, f32[1,256]{1,0:T(1,128)S(1)}, u32[]{:S(2)}, u32[]{:S(2)}) collective-permute-start(f32[1,256]{1,0:T(1,128)} %get-tuple-element.9), channel_id=1, source_target_pairs={{0,1},{1,2},{2,3},{4,5},{5,6},{6,7},{8,9},{9,10},{10,11},{12,13},{... | collective-permute-start | bytes 3080 | tf_op jit(solution)/shard_map/ppermute | solution.py:223
  97.0 5.7 %collective-permute-start.1 = (f32[1,256]{1,0:T(1,128)}, f32[1,256]{1,0:T(1,128)S(1)}, u32[]{:S(2)}, u32[]{:S(2)}) collective-permute-start(f32[1,256]{1,0:T(1,128)} %get-tuple-element.10), channel_id=1, source_target_pairs={{1,0},{2,1},{3,2},{5,4},{6,5},{7,6},{9,8},{10,9},{11,10},{13,12},{... | collective-permute-start | bytes 3080 | tf_op jit(solution)/shard_map/ppermute | solution.py:224
  99.3 3.3 %copy-start.4 = (f32[1,256]{1,0:T(1,128)}, f32[1,256]{1,0:T(1,128)S(1)}, u32[]{:S(2)}) copy-start(f32[1,256]{1,0:T(1,128)S(1)} %collective-permute-done.from_left) | copy-start | bytes 3076
  102.6 0.6 copy-start.5

commit v2 on v1

--- a/solution.py
+++ b/solution.py
@@ -12,8 +12,9 @@
 SPAN = 32
 
 
-def arrange(meta, first, second, out, rows):
-    for view, source in enumerate((first, second)):
+def arrange(meta, *refs):
+    *sources, out, rows = refs
+    for view, source in enumerate(sources):
         for chan in range(CG):
             rows[...] = source[0, chan].astype(jnp.float32)
             for block in range(ZH):
@@ -22,21 +23,23 @@
                     out[block * ZL + phase, view, chan] = picked.astype(jnp.bfloat16)
 
 
-def arrange_call(meta, arrived):
-    spec = pl.BlockSpec((1, CG, 160, 128), lambda i, m: (m[0], 0, 0, 0))
-    spec_b = pl.BlockSpec((1, CG, 160, 128), lambda i, m: (m[1], 0, 0, 0))
+def arrange_call(meta, arrived, picks):
+    def spec(pick):
+        return pl.BlockSpec((1, CG, 160, 128), lambda i, m: (m[pick], 0, 0, 0))
+
+    shape = (16, len(picks), CG, 16, 128)
     return pl.pallas_call(
         arrange,
         grid_spec=pltpu.PrefetchScalarGridSpec(
             num_scalar_prefetch=1,
             grid=(1,),
-            in_specs=[spec, spec_b],
-            out_specs=pl.BlockSpec((16, 2, CG, 16, 128), lambda i, m: (0, 0, 0, 0, 0)),
+            in_specs=[spec(pick) for pick in picks],
+            out_specs=pl.BlockSpec(shape, lambda i, m: (0, 0, 0, 0, 0)),
             scratch_shapes=[pltpu.VMEM((160, 128), jnp.float32)],
         ),
-        out_shape=jax.ShapeDtypeStruct((16, 2, CG, 16, 128), jnp.bfloat16),
+        out_shape=jax.ShapeDtypeStruct(shape, jnp.bfloat16),
         name="arrange",
-    )(meta, arrived, arrived)
+    )(meta, *[arrived] * len(picks))
 
 
 def products(meta, first, second, ref, out, rows, refs):
@@ -58,7 +61,8 @@
 
 def products_call(meta, arrived, ref):
     def spec(view):
-        return pl.BlockSpec((1, 1, CG, 16, 128), lambda i, m: (m[2 + view], view, 0, 0, 0))
+        slot = view if arrived.shape[1] == 2 else 0
+        return pl.BlockSpec((1, 1, CG, 16, 128), lambda i, m: (m[2 + view], slot, 0, 0, 0))
 
     return pl.pallas_call(
         products,
@@ -205,18 +209,28 @@
     )(cost, from_left, from_right)
 
 
+def spread(meta, arrived, ref_feats, picks):
+    windows = arrange_call(meta, arrived, picks)
+    windows = lax.all_to_all(windows, ("zh", "zl"), 0, 0, tiled=True)
+    return products_call(meta, windows, ref_feats)
+
+
 def body(ref_feats, crops, owner, offsets, bands, taps, filt):
     block = lax.axis_index("zh")
     phase = lax.axis_index("zl")
     group = lax.axis_index("x") * NC + lax.axis_index("c")
     near = owner % G
     far = owner // G
-    meta = jnp.stack([near[0], near[1], far[0], far[1], block, phase, group]).astype(jnp.int32)
+    mine = jnp.where(far[1] == block * ZL + phase, near[1], near[0])
+    meta = jnp.stack([near[0], near[1], far[0], far[1], block, phase, group, mine]).astype(jnp.int32)
     arrived = lax.all_to_all(crops[0], ("x", "c"), 0, 0, tiled=True)
     weights = weigh_call(meta, offsets, bands, taps)
-    windows = arrange_call(meta, arrived.reshape(G, CG, 160, 128))
-    windows = lax.all_to_all(windows, ("zh", "zl"), 0, 0, tiled=True)
-    pieces = products_call(meta, windows, ref_feats)
+    arrived = arrived.reshape(G, CG, 160, 128)
+    pieces = lax.cond(
+        far[0] == far[1],
+        lambda: spread(meta, arrived, ref_feats, (0, 1)),
+        lambda: spread(meta, arrived, ref_feats, (7,)),
+    )
     pieces = lax.all_to_all(pieces, ("zl", "x", "c"), 0, 0, tiled=True)
     cost, right, left = filtered_call(filt.reshape(G * 9), weights, pieces)
     count = lax.axis_size("ta")

time: 105 us -> 92.2 us (0.88)
  blocking collectives: 44.1 us -> 33.6 us
  waiting for transfers between devices: 27.9 us -> 24.6 us
  between operations: 0.07 us -> 3.22 us
  Pallas kernels: 12.6 us -> 10.8 us
    all_to_all x1, blocking collectives: 44.1 us -> 33.6 us  [spread(): windows = lax.all_to_all(windows, ('zh', 'zl'), 0, 0, tiled=True)]
    all_to_all x1, waiting for transfers between devices: 18.2 us -> 14.9 us  [body(): arrived = lax.all_to_all(crops[0], ('x', 'c'), 0, 0, tiled=True)]
    pallas_call x1, Pallas kernels: 2.59 us -> 1.29 us  [arrange_call(): pl.pallas_call(arrange, grid_spec=pltpu.PrefetchScalarGridSpec(num_scalar...]
    unnamed x16, local copies, waits for them, and re-layouts: 3.32 us -> 2.27 us
  transfers between devices with their start and end apart: 4 -> 4, of which waited for: 3 -> 3; matrix products, arithmetic and copies ran while one was open for 2% -> 3% of each run, Pallas kernels for 3% -> 3%
where the time goes in v2:
time: 92.2 us; the launch traced here: 91.5 us
  blocking collectives  33.6 us (36%)
  waiting for transfers between devices  24.6 us (27%)
  starting transfers between devices  15.6 us (17%)
  Pallas kernels  10.8 us (12%)
  local copies, waits for them, and re-layouts  3.65 us (4%)
  between operations  3.22 us (3%)
    all_to_all x1, blocking collectives, spread(): windows = lax.all_to_all(windows, ('zh', 'zl'), 0, 0, tiled=True)  33.6 us
    all_to_all x1, waiting for transfers between devices, body(): arrived = lax.all_to_all(crops[0], ('x', 'c'), 0, 0, tiled=True)  14.9 us
    all_to_all x1, waiting for transfers between devices, body(): pieces = lax.all_to_all(pieces, ('zl', 'x', 'c'), 0, 0, tiled=True)  6.59 us
    all_to_all x1, starting transfers between devices, body(): pieces = lax.all_to_all(pieces, ('zl', 'x', 'c'), 0, 0, tiled=True)  5.31 us
    all_to_all x1, starting transfers between devices, body(): arrived = lax.all_to_all(crops[0], ('x', 'c'), 0, 0, tiled=True)  4.43 us
    ppermute x1, starting transfers between devices, body(): lax.ppermute(right, 'ta', [(i, i + 1) for i in range(count - 1)])  3.48 us
    ppermute x1, waiting for transfers between devices, body(): lax.ppermute(left, 'ta', [(i + 1, i) for i in range(count - 1)])  3.14 us
    pallas_call x1, Pallas kernels, filtered_call(): pl.pallas_call(filtered, in_specs=[pl.BlockSpec(memory_space=pltpu.SMEM),...  2.96 us
  transfers between devices with their start and end apart: 4, of which 3 were waited for; matrix products, arithmetic and copies ran while one was open for 3% of the time, Pallas kernels for 3%

profile of v2, /device:TPU:8, one launch (start us, length us, event | category | flops | bytes accessed | tf_op | source)
XLA Modules:
  0.0 91.5 jit_solution(9759733635526975760)
XLA Ops:
  0.0 0.0 copy-start.6
  0.0 0.0 copy-start
  0.0 4.4 %all-to-all-start.2 = ((bf16[32,160,128]{2,1,0:T(8,128)(2,1)}), bf16[32,160,128]{2,1,0:T(8,128)(2,1)S(1)}, u32[]{:S(2)}, u32[]{:S(2)}) async-start(bf16[32,160,128]{2,1,0:T(8,128)(2,1)} %bitcast.12), calls=%async_computation.2 | async-start | bytes 2621440 | tf_op jit(solution)/shard_map/all_to_all | solution.py:226
  4.4 0.0 copy-done.6
  4.5 0.7 fusion
  8.3 0.1 stack.19.meta
  8.4 14.9 %all-to-all-done.2 = bf16[32,160,128]{2,1,0:T(8,128)(2,1)S(1)} async-done(((bf16[32,160,128]{2,1,0:T(8,128)(2,1)}), bf16[32,160,128]{2,1,0:T(8,128)(2,1)S(1)}, u32[]{:S(2)}, u32[]{:S(2)}) %all-to-all-start.2) | async-done | bytes 1310752 | tf_op jit(solution)/shard_map/all_to_all | solution.py:226
  23.2 0.0 copy-done
  23.2 0.0 copy-start.3
  23.2 0.0 copy-start.2
  23.2 37.0 %conditional.1 = (f32[32,2,8,128]{3,2,1,0:T(8,128)}) conditional(s32[]{:T(128)} %convert_element_type.3, (s32[8]{0:T(128)S(1)}, bf16[8,4,160,128]{3,2,1,0:T(8,128)(2,1)S(1)}, bf16[32,128,128]{2,1,0:T(8,128)(2,1)S(1)}) %tuple.21, (s32[8]{0:T(128)S(1)}, bf16[8,4,160,128]{3,2,1,0:T(8,128)(2,1)S(1)}, bf16[32,128,128]{2,1,0:T(8,128)(2,1)S(1)}) %tuple.22), branch_computations={%region_0.1_spmd, %region_1.2_spmd} | conditional | bytes 1048584 | solution.py:229
  23.2 1.3 %arrange.2 = bf16[16,1,4,16,128]{4,3,2,1,0:T(8,128)(2,1)} custom-call(s32[8]{0:T(128)S(1)} %get-tuple-element.20.meta, bf16[8,4,160,128]{3,2,1,0:T(8,128)(2,1)S(1)} %get-tuple-element.21.refs_0_), custom_call_target="tpu_custom_call" | custom-call | tf_op jit(solution)/shard_map/cond/branch_0_fun/arrange/pallas_call | solution.py:31
  24.5 33.6 %all_to_all.18.first.second = bf16[16,1,4,16,128]{4,3,2,1,0:T(8,128)(2,1)} all-to-all(bf16[16,1,4,16,128]{4,3,2,1,0:T(8,128)(2,1)} %arrange.2), channel_id=1, replica_groups=mesh['zh'=4,'zl'=4,'x'=4,'c'=2,'ta'=4] {'zh','zl'}, dimensions={0} | all-to-all | bytes 524288 | tf_op jit(solution)/shard_map/cond/branch_0_fun/all_to_all | solution.py:214
  58.1 2.1 %products.2 = f32[32,2,8,128]{3,2,1,0:T(8,128)} custom-call(s32[8]{0:T(128)S(1)} %get-tuple-element.20.meta, bf16[16,1,4,16,128]{4,3,2,1,0:T(8,128)(2,1)} %all_to_all.18.first.second, bf16[16,1,4,16,128]{4,3,2,1,0:T(8,128)(2,1)} %all_to_all.18.first.second, bf16[32,128,128]{2,1,0:T(8,128)(2,1)S(1)} %get-tuple-element.22.ref), custom_call_target="tpu_custom_call" | custom-call | tf_op jit(solution)/shard_map/cond/branch_0_fun/products/pallas_call | solution.py:67
  60.2 5.3 %all-to-all-start.3 = ((f32[32,2,8,128]{3,2,1,0:T(8,128)}), f32[32,2,8,128]{3,2,1,0:T(8,128)S(1)}, u32[]{:S(2)}, u32[]{:S(2)}) async-start(f32[32,2,8,128]{3,2,1,0:T(8,128)} %get-tuple-element.40), calls=%async_computation.3 | async-start | bytes 524288 | tf_op jit(solution)/shard_map/all_to_all | solution.py:234
  65.5 0.0 copy-done.3
  65.6 0.1 copy.10
  65.7 0.6 reshape.6.filt
  66.3 0.0 copy-done.2
  66.3 0.9 copy.11.taps
  67.1 2.9 %weigh.1.weights = bf16[256,256]{1,0:T(8,128)(2,1)} custom-call(s32[8]{0:T(128)S(1)} %stack.19.meta, s32[2,256]{1,0:T(2,128)} %offsets.1, s32[2,256]{1,0:T(2,128)} %bands.1, f32[2,256,4]{2,1,0:T(8,128)} %copy.11.taps), custom_call_target="tpu_custom_call" | custom-call | tf_op jit(solution)/shard_map/weigh/pallas_call | solution.py:114
  70.1 6.6 %all-to-all-done.3.pieces = f32[32,2,8,128]{3,2,1,0:T(8,128)S(1)} async-done(((f32[32,2,8,128]{3,2,1,0:T(8,128)}), f32[32,2,8,128]{3,2,1,0:T(8,128)S(1)}, u32[]{:S(2)}, u32[]{:S(2)}) %all-to-all-start.3) | async-done | bytes 262176 | tf_op jit(solution)/shard_map/all_to_all | solution.py:234
  76.6 0.0 copy-start.1
  76.6 0.7 copy-done.1
  77.4 3.0 %filtered.1 = (f32[256,128]{1,0:T(8,128)}, f32[1,256]{1,0:T(1,128)}, f32[1,256]{1,0:T(1,128)}) custom-call(f32[72]{0:T(128)} %reshape.6.filt, bf16[256,256]{1,0:T(8,128)(2,1)} %weigh.1.weights, f32[32,2,8,128]{3,2,1,0:T(8,128)} %copy-done.1), custom_call_target="tpu_custom_call" | custom-call | tf_op jit(solution)/shard_map/filtered/pallas_call | solution.py:177
  80.3 3.5 %collective-permute-start = (f32[1,256]{1,0:T(1,128)}, f32[1,256]{1,0:T(1,128)S(1)}, u32[]{:S(2)}, u32[]{:S(2)}) collective-permute-start(f32[1,256]{1,0:T(1,128)} %get-tuple-element.30), channel_id=1, source_target_pairs={{0,1},{1,2},{2,3},{4,5},{5,6},{6,7},{8,9},{9,10},{10,11},{12,13},{... | collective-permute-start | bytes 3080 | tf_op jit(solution)/shard_map/ppermute | solution.py:237
  83.8 2.4 %collective-permute-start.1 = (f32[1,256]{1,0:T(1,128)}, f32[1,256]{1,0:T(1,128)S(1)}, u32[]{:S(2)}, u32[]{:S(2)}) collective-permute-start(f32[1,256]{1,0:T(1,128)} %get-tuple-element.31), channel_id=1, source_target_pairs={{1,0},{2,1},{3,2},{5,4},{6,5},{7,6},{9,8},{10,9},{11,10},{13,12},{... | collective-permute-start | bytes 3080 | tf_op jit(solution)/shard_map/ppermute | solution.py:238
  86.2 0.0 collective-permute-done.from_left
  86.2 0.0 copy-start.4
  86.2 3.1 %collective-permute-done.1.from_right = f32[1,256]{1,0:T(1,128)S(1)} collective-permute-done((f32[1,256]{1,0:T(1,128)}, f32[1,256]{1,0:T(1,128)S(1)}, u32[]{:S(2)}, u32[]{:S(2)}) %collective-permute-start.1) | collective-permute-done | bytes 1056 | tf_op jit(solution)/shard_map/ppermute | solution.py:238
  89.3 0.0 copy-start.5
  89.3 0.0 copy-done.4
  89.3 0.6 copy-done.5
  89.9 1.6 %expected.1 = f32[1,128]{1,0:T(1,128)} custom-call(f32[256,128]{1,0:T(8,128)} %get-tuple-element.29.cost, f32[1,256]{1,0:T(1,128)} %copy-done.4, f32[1,256]{1,0:T(1,128)} %copy-done.5), custom_call_target="tpu_custom_call" | custom-call | tf_op jit(solution)/shard_map/expected/pallas_call | solution.py:205
  (1 shorter events, 0.0 us)
Async XLA Ops:
  0.0 4.4 %copy-start.6 = (s32[2]{0:T(128)S(1)}, s32[2]{0:T(128)}, u32[]{:S(2)}) copy-start(s32[2]{0:T(128)} %param.11) | copy-start | bytes 28
  0.0 23.2 %copy-start = (bf16[32,128,128]{2,1,0:T(8,128)(2,1)S(1)}, bf16[32,128,128]{2,1,0:T(8,128)(2,1)}, u32[]{:S(2)}) copy-start(bf16[32,128,128]{2,1,0:T(8,128)(2,1)} %param.9) | copy-start | bytes 3145732
  0.0 23.2 %all-to-all-start.2 = ((bf16[32,160,128]{2,1,0:T(8,128)(2,1)}), bf16[32,160,128]{2,1,0:T(8,128)(2,1)S(1)}, u32[]{:S(2)}, u32[]{:S(2)}) async-start(bf16[32,160,128]{2,1,0:T(8,128)(2,1)} %bitcast.12), calls=%async_computation.2 | async-start | bytes 2621440 | tf_op jit(solution)/shard_map/all_to_all | solution.py:226
  23.2 42.3 %copy-start.3 = (f32[8,3,3]{0,2,1:T(4,128)S(1)}, f32[8,3,3]{0,2,1:T(4,128)}, u32[]{:S(2)}) copy-start(f32[8,3,3]{0,2,1:T(4,128)} %param.15) | copy-start | bytes 868
  23.2 43.1 %copy-start.2 = (f32[2,256,4]{1,2,0:T(4,128)S(1)}, f32[2,256,4]{1,2,0:T(4,128)}, u32[]{:S(2)}) copy-start(f32[2,256,4]{1,2,0:T(4,128)} %param.14) | copy-start | bytes 24580
  60.2 16.4 %all-to-all-start.3 = ((f32[32,2,8,128]{3,2,1,0:T(8,128)}), f32[32,2,8,128]{3,2,1,0:T(8,128)S(1)}, u32[]{:S(2)}, u32[]{:S(2)}) async-start(f32[32,2,8,128]{3,2,1,0:T(8,128)} %get-tuple-element.40), calls=%async_computation.3 | async-start | bytes 524288 | tf_op jit(solution)/shard_map/all_to_all | solution.py:234
  76.6 0.7 copy-start.1
  80.3 5.8 %collective-permute-start = (f32[1,256]{1,0:T(1,128)}, f32[1,256]{1,0:T(1,128)S(1)}, u32[]{:S(2)}, u32[]{:S(2)}) collective-permute-start(f32[1,256]{1,0:T(1,128)} %get-tuple-element.30), channel_id=1, source_target_pairs={{0,1},{1,2},{2,3},{4,5},{5,6},{6,7},{8,9},{9,10},{10,11},{12,13},{... | collective-permute-start | bytes 3080 | tf_op jit(solution)/shard_map/ppermute | solution.py:237
  83.8 5.5 %collective-permute-start.1 = (f32[1,256]{1,0:T(1,128)}, f32[1,256]{1,0:T(1,128)S(1)}, u32[]{:S(2)}, u32[]{:S(2)}) collective-permute-start(f32[1,256]{1,0:T(1,128)} %get-tuple-element.31), channel_id=1, source_target_pairs={{1,0},{2,1},{3,2},{5,4},{6,5},{7,6},{9,8},{10,9},{11,10},{13,12},{... | collective-permute-start | bytes 3080 | tf_op jit(solution)/shard_map/ppermute | solution.py:238
  86.2 3.2 %copy-start.4 = (f32[1,256]{1,0:T(1,128)}, f32[1,256]{1,0:T(1,128)S(1)}, u32[]{:S(2)}) copy-start(f32[1,256]{1,0:T(1,128)S(1)} %collective-permute-done.from_left) | copy-start | bytes 3076
  89.3 0.6 copy-start.5

commit v3 on v2

--- a/solution.py
+++ b/solution.py
@@ -10,6 +10,10 @@
 D = 256
 ZH, ZL, NX, NC = 4, 4, 4, 2
 SPAN = 32
+
+
+def near_core(array):
+    return pltpu.with_memory_space_constraint(array, pltpu.VMEM)
 
 
 def arrange(meta, *refs):
@@ -37,7 +41,7 @@
             out_specs=pl.BlockSpec(shape, lambda i, m: (0, 0, 0, 0, 0)),
             scratch_shapes=[pltpu.VMEM((160, 128), jnp.float32)],
         ),
-        out_shape=jax.ShapeDtypeStruct(shape, jnp.bfloat16),
+        out_shape=pltpu.VMEM(shape, jnp.bfloat16),
         name="arrange",
     )(meta, *[arrived] * len(picks))
 
@@ -80,7 +84,7 @@
                 pltpu.VMEM((CG, SPAN, 128), jnp.float32),
             ],
         ),
-        out_shape=jax.ShapeDtypeStruct((SPAN, 2, 8, 128), jnp.float32),
+        out_shape=pltpu.VMEM((SPAN, 2, 8, 128), jnp.float32),
         name="products",
     )(meta, arrived, arrived, ref)
 
@@ -123,7 +127,7 @@
             ],
             out_specs=pl.BlockSpec((D, 256), lambda i, m: (0, 0)),
         ),
-        out_shape=jax.ShapeDtypeStruct((D, 256), jnp.bfloat16),
+        out_shape=pltpu.VMEM((D, 256), jnp.bfloat16),
         name="weigh",
     )(meta, offsets, bands, taps)
 
@@ -173,7 +177,7 @@
 
 
 def filtered_call(filt, weights, pieces):
-    edge = jax.ShapeDtypeStruct((1, D), jnp.float32)
+    edge = pltpu.VMEM((1, D), jnp.float32)
     return pl.pallas_call(
         filtered,
         in_specs=[
@@ -181,7 +185,7 @@
             pl.BlockSpec(memory_space=pltpu.VMEM),
             pl.BlockSpec(memory_space=pltpu.VMEM),
         ],
-        out_shape=[jax.ShapeDtypeStruct((D, 128), jnp.float32), edge, edge],
+        out_shape=[pltpu.VMEM((D, 128), jnp.float32), edge, edge],
         scratch_shapes=[
             pltpu.VMEM((256, 1024), jnp.bfloat16),
             pltpu.VMEM((D, 1024), jnp.float32),
@@ -212,7 +216,7 @@
 def spread(meta, arrived, ref_feats, picks):
     windows = arrange_call(meta, arrived, picks)
     windows = lax.all_to_all(windows, ("zh", "zl"), 0, 0, tiled=True)
-    return products_call(meta, windows, ref_feats)
+    return products_call(meta, near_core(windows), ref_feats)
 
 
 def body(ref_feats, crops, owner, offsets, bands, taps, filt):
@@ -225,18 +229,18 @@
     meta = jnp.stack([near[0], near[1], far[0], far[1], block, phase, group, mine]).astype(jnp.int32)
     arrived = lax.all_to_all(crops[0], ("x", "c"), 0, 0, tiled=True)
     weights = weigh_call(meta, offsets, bands, taps)
-    arrived = arrived.reshape(G, CG, 160, 128)
+    arrived = near_core(arrived.reshape(G, CG, 160, 128))
     pieces = lax.cond(
         far[0] == far[1],
         lambda: spread(meta, arrived, ref_feats, (0, 1)),
         lambda: spread(meta, arrived, ref_feats, (7,)),
     )
     pieces = lax.all_to_all(pieces, ("zl", "x", "c"), 0, 0, tiled=True)
-    cost, right, left = filtered_call(filt.reshape(G * 9), weights, pieces)
+    cost, right, left = filtered_call(filt.reshape(G * 9), near_core(weights), near_core(pieces))
     count = lax.axis_size("ta")
     from_left = lax.ppermute(right, "ta", [(i, i + 1) for i in range(count - 1)])
     from_right = lax.ppermute(left, "ta", [(i + 1, i) for i in range(count - 1)])
-    return expected_call(cost, from_left, from_right)
+    return expected_call(near_core(cost), near_core(from_left), near_core(from_right))
 
 
 def solution(mesh):

time: 92.2 us -> 86.9 us (0.943)
  Pallas kernels: 10.8 us -> 6.88 us
  local copies, waits for them, and re-layouts: 3.65 us -> 2.33 us
    unnamed x16 -> x10, local copies, waits for them, and re-layouts: 2.27 us -> 0.96 us
    pallas_call x1, Pallas kernels: 2.96 us -> 2 us  [filtered_call(): pl.pallas_call(filtered, in_specs=[pl.BlockSpec(memory_space=pltpu.SMEM),...]
where the time goes in v3:
time: 86.9 us; the launch traced here: 86.6 us
  blocking collectives  33.3 us (38%)
  waiting for transfers between devices  25.1 us (29%)
  starting transfers between devices  15.6 us (18%)
  Pallas kernels  6.88 us (8%)
  between operations  3.27 us (4%)
  local copies, waits for them, and re-layouts  2.33 us (3%)
    all_to_all x1, blocking collectives, spread(): windows = lax.all_to_all(windows, ('zh', 'zl'), 0, 0, tiled=True)  33.3 us
    all_to_all x1, waiting for transfers between devices, body(): arrived = lax.all_to_all(crops[0], ('x', 'c'), 0, 0, tiled=True)  14.8 us
    all_to_all x1, waiting for transfers between devices, body(): pieces = lax.all_to_all(pieces, ('zl', 'x', 'c'), 0, 0, tiled=True)  7.25 us
    all_to_all x1, starting transfers between devices, body(): pieces = lax.all_to_all(pieces, ('zl', 'x', 'c'), 0, 0, tiled=True)  5.31 us
    all_to_all x1, starting transfers between devices, body(): arrived = lax.all_to_all(crops[0], ('x', 'c'), 0, 0, tiled=True)  4.43 us
    ppermute x1, starting transfers between devices, body(): lax.ppermute(right, 'ta', [(i, i + 1) for i in range(count - 1)])  3.49 us
    ppermute x1, waiting for transfers between devices, body(): lax.ppermute(left, 'ta', [(i + 1, i) for i in range(count - 1)])  3.09 us
    ppermute x1, starting transfers between devices, body(): lax.ppermute(left, 'ta', [(i + 1, i) for i in range(count - 1)])  2.35 us
  transfers between devices with their start and end apart: 4, of which 3 were waited for; matrix products, arithmetic and copies ran while one was open for 3% of the time, Pallas kernels for 3%

profile of v3, /device:TPU:8, one launch (start us, length us, event | category | flops | bytes accessed | tf_op | source)
XLA Modules:
  0.0 86.6 jit_solution(16124294927946155625)
XLA Ops:
  0.0 0.0 copy-start.5
  0.0 0.0 copy-start
  0.0 4.4 %all-to-all-start.2 = ((bf16[32,160,128]{2,1,0:T(8,128)(2,1)}), bf16[32,160,128]{2,1,0:T(8,128)(2,1)S(1)}, u32[]{:S(2)}, u32[]{:S(2)}) async-start(bf16[32,160,128]{2,1,0:T(8,128)(2,1)} %bitcast.12), calls=%async_computation.2 | async-start | bytes 2621440 | tf_op jit(solution)/shard_map/all_to_all | solution.py:230
  4.4 0.0 copy-done.5
  4.5 0.7 fusion
  8.3 0.1 stack.19.meta
  8.4 14.8 %all-to-all-done.2 = bf16[32,160,128]{2,1,0:T(8,128)(2,1)S(1)} async-done(((bf16[32,160,128]{2,1,0:T(8,128)(2,1)}), bf16[32,160,128]{2,1,0:T(8,128)(2,1)S(1)}, u32[]{:S(2)}, u32[]{:S(2)}) %all-to-all-start.2) | async-done | bytes 1310752 | tf_op jit(solution)/shard_map/all_to_all | solution.py:230
  23.2 0.0 copy-done
  23.2 0.0 copy-start.4
  23.2 0.0 copy-start.3
  23.2 35.3 %conditional.1 = (f32[32,2,8,128]{3,2,1,0:T(8,128)}) conditional(s32[]{:T(128)} %convert_element_type.3, (s32[8]{0:T(128)S(1)}, bf16[8,4,160,128]{3,2,1,0:T(8,128)(2,1)S(1)}, bf16[32,128,128]{2,1,0:T(8,128)(2,1)S(1)}) %tuple.21, (s32[8]{0:T(128)S(1)}, bf16[8,4,160,128]{3,2,1,0:T(8,128)(2,1)S(1)}, bf16[32,128,128]{2,1,0:T(8,128)(2,1)S(1)}) %tuple.22), branch_computations={%region_0.1_spmd, %region_1.2_spmd} | conditional | bytes 9437248 | solution.py:233
  23.2 0.6 arrange.2
  23.8 33.3 %all_to_all.18.first.second = bf16[16,1,4,16,128]{4,3,2,1,0:T(8,128)(2,1)S(1)} all-to-all(bf16[16,1,4,16,128]{4,3,2,1,0:T(8,128)(2,1)S(1)} %arrange.2), channel_id=1, replica_groups=mesh['zh'=4,'zl'=4,'x'=4,'c'=2,'ta'=4] {'zh','zl'}, dimensions={0} | all-to-all | bytes 524288 | tf_op jit(solution)/shard_map/cond/branch_0_fun/all_to_all | solution.py:218
  57.2 1.3 %products.2 = f32[32,2,8,128]{3,2,1,0:T(8,128)} custom-call(s32[8]{0:T(128)S(1)} %get-tuple-element.20.meta, bf16[16,1,4,16,128]{4,3,2,1,0:T(8,128)(2,1)S(1)} %all_to_all.18.first.second, bf16[16,1,4,16,128]{4,3,2,1,0:T(8,128)(2,1)S(1)} %all_to_all.18.first.second, bf16[32,128,128]{2,1,0:T(8,128)(2,1)S(1)} %get-tuple-element.22.ref), custom_call_target="tpu_custom_call" | custom-call | tf_op jit(solution)/shard_map/cond/branch_0_fun/products/pallas_call | solution.py:71
  58.5 5.3 %all-to-all-start.3 = ((f32[32,2,8,128]{3,2,1,0:T(8,128)}), f32[32,2,8,128]{3,2,1,0:T(8,128)S(1)}, u32[]{:S(2)}, u32[]{:S(2)}) async-start(f32[32,2,8,128]{3,2,1,0:T(8,128)} %get-tuple-element.40), calls=%async_computation.3 | async-start | bytes 524288 | tf_op jit(solution)/shard_map/all_to_all | solution.py:238
  63.8 0.0 copy-done.4
  63.8 0.1 copy.10
  63.9 0.6 reshape.6.filt
  64.5 0.0 copy-done.3
  64.5 0.8 copy.11.taps
  65.4 2.3 %weigh.1.weights = bf16[256,256]{1,0:T(8,128)(2,1)S(1)} custom-call(s32[8]{0:T(128)S(1)} %stack.19.meta, s32[2,256]{1,0:T(2,128)} %offsets.1, s32[2,256]{1,0:T(2,128)} %bands.1, f32[2,256,4]{2,1,0:T(8,128)} %copy.11.taps), custom_call_target="tpu_custom_call" | custom-call | tf_op jit(solution)/shard_map/weigh/pallas_call | solution.py:118
  67.7 7.3 %all-to-all-done.3.pieces = f32[32,2,8,128]{3,2,1,0:T(8,128)S(1)} async-done(((f32[32,2,8,128]{3,2,1,0:T(8,128)}), f32[32,2,8,128]{3,2,1,0:T(8,128)S(1)}, u32[]{:S(2)}, u32[]{:S(2)}) %all-to-all-start.3) | async-done | bytes 262176 | tf_op jit(solution)/shard_map/all_to_all | solution.py:238
  74.9 2.0 %filtered.1 = (f32[256,128]{1,0:T(8,128)S(1)}, f32[1,256]{1,0:T(1,128)S(1)}, f32[1,256]{1,0:T(1,128)S(1)}) custom-call(f32[72]{0:T(128)} %reshape.6.filt, bf16[256,256]{1,0:T(8,128)(2,1)S(1)} %weigh.1.weights, f32[32,2,8,128]{3,2,1,0:T(8,128)S(1)} %all-to-all-done.3.pieces), custom_call_target="tpu_custom_call" | custom-call | tf_op jit(solution)/shard_map/filtered/pallas_call | solution.py:181
  76.9 3.5 %collective-permute-start = (f32[1,256]{1,0:T(1,128)S(1)}, f32[1,256]{1,0:T(1,128)S(1)}, u32[]{:S(2)}, u32[]{:S(2)}) collective-permute-start(f32[1,256]{1,0:T(1,128)S(1)} %get-tuple-element.30), channel_id=1, source_target_pairs={{0,1},{1,2},{2,3},{4,5},{5,6},{6,7},{8,9},{9,10},{10,11},{12,13},{... | collective-permute-start | bytes 3080 | tf_op jit(solution)/shard_map/ppermute | solution.py:241
  80.4 2.4 %collective-permute-start.1 = (f32[1,256]{1,0:T(1,128)S(1)}, f32[1,256]{1,0:T(1,128)S(1)}, u32[]{:S(2)}, u32[]{:S(2)}) collective-permute-start(f32[1,256]{1,0:T(1,128)S(1)} %get-tuple-element.31), channel_id=1, source_target_pairs={{1,0},{2,1},{3,2},{5,4},{6,5},{7,6},{9,8},{10,9},{11,10},{13,12},{... | collective-permute-start | bytes 3080 | tf_op jit(solution)/shard_map/ppermute | solution.py:242
  82.8 0.0 collective-permute-done.from_left
  82.8 3.1 %collective-permute-done.1.from_right = f32[1,256]{1,0:T(1,128)S(1)} collective-permute-done((f32[1,256]{1,0:T(1,128)S(1)}, f32[1,256]{1,0:T(1,128)S(1)}, u32[]{:S(2)}, u32[]{:S(2)}) %collective-permute-start.1) | collective-permute-done | bytes 1056 | tf_op jit(solution)/shard_map/ppermute | solution.py:242
  85.9 0.7 expected.1
  (1 shorter events, 0.0 us)
Async XLA Ops:
  0.0 4.4 %copy-start.5 = (s32[2]{0:T(128)S(1)}, s32[2]{0:T(128)}, u32[]{:S(2)}) copy-start(s32[2]{0:T(128)} %param.11) | copy-start | bytes 28
  0.0 23.2 %copy-start = (bf16[32,128,128]{2,1,0:T(8,128)(2,1)S(1)}, bf16[32,128,128]{2,1,0:T(8,128)(2,1)}, u32[]{:S(2)}) copy-start(bf16[32,128,128]{2,1,0:T(8,128)(2,1)} %param.9) | copy-start | bytes 3145732
  0.0 23.2 %all-to-all-start.2 = ((bf16[32,160,128]{2,1,0:T(8,128)(2,1)}), bf16[32,160,128]{2,1,0:T(8,128)(2,1)S(1)}, u32[]{:S(2)}, u32[]{:S(2)}) async-start(bf16[32,160,128]{2,1,0:T(8,128)(2,1)} %bitcast.12), calls=%async_computation.2 | async-start | bytes 2621440 | tf_op jit(solution)/shard_map/all_to_all | solution.py:230
  23.2 40.6 %copy-start.4 = (f32[8,3,3]{0,2,1:T(4,128)S(1)}, f32[8,3,3]{0,2,1:T(4,128)}, u32[]{:S(2)}) copy-start(f32[8,3,3]{0,2,1:T(4,128)} %param.15) | copy-start | bytes 868
  23.2 41.3 %copy-start.3 = (f32[2,256,4]{1,2,0:T(4,128)S(1)}, f32[2,256,4]{1,2,0:T(4,128)}, u32[]{:S(2)}) copy-start(f32[2,256,4]{1,2,0:T(4,128)} %param.14) | copy-start | bytes 24580
  58.5 16.4 %all-to-all-start.3 = ((f32[32,2,8,128]{3,2,1,0:T(8,128)}), f32[32,2,8,128]{3,2,1,0:T(8,128)S(1)}, u32[]{:S(2)}, u32[]{:S(2)}) async-start(f32[32,2,8,128]{3,2,1,0:T(8,128)} %get-tuple-element.40), calls=%async_computation.3 | async-start | bytes 524288 | tf_op jit(solution)/shard_map/all_to_all | solution.py:238
  76.9 5.9 %collective-permute-start = (f32[1,256]{1,0:T(1,128)S(1)}, f32[1,256]{1,0:T(1,128)S(1)}, u32[]{:S(2)}, u32[]{:S(2)}) collective-permute-start(f32[1,256]{1,0:T(1,128)S(1)} %get-tuple-element.30), channel_id=1, source_target_pairs={{0,1},{1,2},{2,3},{4,5},{5,6},{6,7},{8,9},{9,10},{10,11},{12,13},{... | collective-permute-start | bytes 3080 | tf_op jit(solution)/shard_map/ppermute | solution.py:241
  80.4 5.5 %collective-permute-start.1 = (f32[1,256]{1,0:T(1,128)S(1)}, f32[1,256]{1,0:T(1,128)S(1)}, u32[]{:S(2)}, u32[]{:S(2)}) collective-permute-start(f32[1,256]{1,0:T(1,128)S(1)} %get-tuple-element.31), channel_id=1, source_target_pairs={{1,0},{2,1},{3,2},{5,4},{6,5},{7,6},{9,8},{10,9},{11,10},{13,12},{... | collective-permute-start | bytes 3080 | tf_op jit(solution)/shard_map/ppermute | solution.py:242

commit v4 on v3

--- a/solution.py
+++ b/solution.py
@@ -132,7 +132,53 @@
     )(meta, offsets, bands, taps)
 
 
-def filtered(filt, weights, pieces, cost, right, left, stack, volume, sums):
+def brink(filt, weights, pieces, right, left, stack, sums):
+    lane = lax.broadcasted_iota(jnp.int32, (16, 128), 1)
+    for block in range(ZL):
+        ends = jnp.zeros((16, 128), jnp.float32)
+        for group in range(G):
+            piece = pieces[block * G + group].reshape(16, 128)
+            ends = jnp.where(lane == group, pltpu.roll(piece, group + 1, 1), ends)
+            ends = jnp.where(lane == G + group, pltpu.roll(piece, G + group, 1), ends)
+        high = ends.astype(jnp.bfloat16)
+        low = (ends - high.astype(jnp.float32)).astype(jnp.bfloat16)
+        for copy in range(2):
+            at = 128 * copy + 16 * block
+            stack[at : at + 16, :] = high
+            stack[at + 64 : at + 80, :] = low
+    part = jnp.dot(weights[...], stack[...], preferred_element_type=jnp.float32) * 0.125
+    part = part.astype(jnp.bfloat16).astype(jnp.float32)
+    slot = lax.broadcasted_iota(jnp.int32, (1, 128), 1)
+    zero = jnp.zeros((8, 128), jnp.float32)
+    for i in range(3):
+        line = jnp.zeros((1, 128), jnp.float32)
+        for group in range(G):
+            line = jnp.where(slot == group, filt[group * 9 + i * 3], line)
+            line = jnp.where(slot == G + group, filt[group * 9 + i * 3 + 2], line)
+        sums[i, 0:8, :] = zero
+        sums[i, D + 8 : D + 16, :] = zero
+        sums[i, 8 : D + 8, :] = part * line
+    total = (sums[0, 7 : D + 7, :] + sums[1, 8 : D + 8, :] + sums[2, 9 : D + 9, :]).T
+    right[...] = jnp.sum(total[0:G], axis=0, keepdims=True)
+    left[...] = jnp.sum(total[G : 2 * G], axis=0, keepdims=True)
+
+
+def brink_call(filt, weights, pieces):
+    edge = pltpu.VMEM((1, D), jnp.float32)
+    return pl.pallas_call(
+        brink,
+        in_specs=[
+            pl.BlockSpec(memory_space=pltpu.SMEM),
+            pl.BlockSpec(memory_space=pltpu.VMEM),
+            pl.BlockSpec(memory_space=pltpu.VMEM),
+        ],
+        out_shape=[edge, edge],
+        scratch_shapes=[pltpu.VMEM((256, 128), jnp.bfloat16), pltpu.VMEM((3, D + 16, 128), jnp.float32)],
+        name="brink",
+    )(filt, weights, pieces)
+
+
+def filtered(filt, weights, pieces, cost, stack, volume, sums):
     for group in range(G):
         lanes = slice(128 * group, 128 * group + 128)
         for block in range(ZL):
@@ -171,13 +217,9 @@
     before = pltpu.roll(column[0], 1, 1)
     after = pltpu.roll(column[2], 127, 1)
     cost[...] = column[1] + jnp.where(lane == 0, 0.0, before) + jnp.where(lane == 127, 0.0, after)
-    edges = jnp.where(lane == 0, before, after).T
-    right[...] = edges[0:1, :]
-    left[...] = edges[127:128, :]
 
 
 def filtered_call(filt, weights, pieces):
-    edge = pltpu.VMEM((1, D), jnp.float32)
     return pl.pallas_call(
         filtered,
         in_specs=[
@@ -185,7 +227,7 @@
             pl.BlockSpec(memory_space=pltpu.VMEM),
             pl.BlockSpec(memory_space=pltpu.VMEM),
         ],
-        out_shape=[pltpu.VMEM((D, 128), jnp.float32), edge, edge],
+        out_shape=pltpu.VMEM((D, 128), jnp.float32),
         scratch_shapes=[
             pltpu.VMEM((256, 1024), jnp.bfloat16),
             pltpu.VMEM((D, 1024), jnp.float32),
@@ -236,10 +278,14 @@
         lambda: spread(meta, arrived, ref_feats, (7,)),
     )
     pieces = lax.all_to_all(pieces, ("zl", "x", "c"), 0, 0, tiled=True)
-    cost, right, left = filtered_call(filt.reshape(G * 9), near_core(weights), near_core(pieces))
+    filt = filt.reshape(G * 9)
+    weights = near_core(weights)
+    pieces = near_core(pieces)
+    right, left = brink_call(filt, weights, pieces)
     count = lax.axis_size("ta")
     from_left = lax.ppermute(right, "ta", [(i, i + 1) for i in range(count - 1)])
     from_right = lax.ppermute(left, "ta", [(i + 1, i) for i in range(count - 1)])
+    cost = filtered_call(filt, weights, pieces)
     return expected_call(near_core(cost), near_core(from_left), near_core(from_right))
 
 

time: 86.9 us -> 86.1 us (level)
  waiting for transfers between devices: 25.1 us -> 23.2 us
  Pallas kernels: 6.88 us -> 7.95 us
    ppermute x1, waiting for transfers between devices: 3.09 us -> 1.13 us  [body(): lax.ppermute(left, 'ta', [(i + 1, i) for i in range(count - 1)])]
    pallas_call x0 -> x1, Pallas kernels: none -> 1.12 us  [brink_call(): pl.pallas_call(brink, in_specs=[pl.BlockSpec(memory_space=pltpu.SMEM), pl...]
  transfers between devices with their start and end apart: 4 -> 4, of which waited for: 3 -> 3; matrix products, arithmetic and copies ran while one was open for 3% -> 3% of each run, Pallas kernels for 3% -> 5%
where the time goes in v4:
time: 86.1 us; the launch traced here: 85.7 us
  blocking collectives  33.3 us (39%)
  waiting for transfers between devices  23.2 us (27%)
  starting transfers between devices  15.6 us (18%)
  Pallas kernels  7.95 us (9%)
  between operations  3.27 us (4%)
  local copies, waits for them, and re-layouts  2.33 us (3%)
    all_to_all x1, blocking collectives, spread(): windows = lax.all_to_all(windows, ('zh', 'zl'), 0, 0, tiled=True)  33.3 us
    all_to_all x1, waiting for transfers between devices, body(): arrived = lax.all_to_all(crops[0], ('x', 'c'), 0, 0, tiled=True)  14.8 us
    all_to_all x1, waiting for transfers between devices, body(): pieces = lax.all_to_all(pieces, ('zl', 'x', 'c'), 0, 0, tiled=True)  7.25 us
    all_to_all x1, starting transfers between devices, body(): pieces = lax.all_to_all(pieces, ('zl', 'x', 'c'), 0, 0, tiled=True)  5.31 us
    all_to_all x1, starting transfers between devices, body(): arrived = lax.all_to_all(crops[0], ('x', 'c'), 0, 0, tiled=True)  4.43 us
    ppermute x1, starting transfers between devices, body(): lax.ppermute(right, 'ta', [(i, i + 1) for i in range(count - 1)])  3.49 us
    ppermute x1, starting transfers between devices, body(): lax.ppermute(left, 'ta', [(i + 1, i) for i in range(count - 1)])  2.36 us
    pallas_call x1, Pallas kernels, weigh_call(): pl.pallas_call(weigh, grid_spec=pltpu.PrefetchScalarGridSpec(num_scalar_p...  2.27 us
  transfers between devices with their start and end apart: 4, of which 3 were waited for; matrix products, arithmetic and copies ran while one was open for 3% of the time, Pallas kernels for 5%

profile of v4, /device:TPU:8, one launch (start us, length us, event | category | flops | bytes accessed | tf_op | source)
XLA Modules:
  0.0 85.7 jit_solution(14648988194618094493)
XLA Ops:
  0.0 0.0 copy-start.5
  0.0 0.0 copy-start
  0.0 4.4 %all-to-all-start.2 = ((bf16[32,160,128]{2,1,0:T(8,128)(2,1)}), bf16[32,160,128]{2,1,0:T(8,128)(2,1)S(1)}, u32[]{:S(2)}, u32[]{:S(2)}) async-start(bf16[32,160,128]{2,1,0:T(8,128)(2,1)} %bitcast.12), calls=%async_computation.2 | async-start | bytes 2621440 | tf_op jit(solution)/shard_map/all_to_all | solution.py:272
  4.4 0.0 copy-done.5
  4.5 0.7 fusion
  8.3 0.1 stack.19.meta
  8.4 14.8 %all-to-all-done.2 = bf16[32,160,128]{2,1,0:T(8,128)(2,1)S(1)} async-done(((bf16[32,160,128]{2,1,0:T(8,128)(2,1)}), bf16[32,160,128]{2,1,0:T(8,128)(2,1)S(1)}, u32[]{:S(2)}, u32[]{:S(2)}) %all-to-all-start.2) | async-done | bytes 1310752 | tf_op jit(solution)/shard_map/all_to_all | solution.py:272
  23.2 0.0 copy-done
  23.2 0.0 copy-start.4
  23.2 0.0 copy-start.3
  23.2 35.3 %conditional.1 = (f32[32,2,8,128]{3,2,1,0:T(8,128)}) conditional(s32[]{:T(128)} %convert_element_type.3, (s32[8]{0:T(128)S(1)}, bf16[8,4,160,128]{3,2,1,0:T(8,128)(2,1)S(1)}, bf16[32,128,128]{2,1,0:T(8,128)(2,1)S(1)}) %tuple.21, (s32[8]{0:T(128)S(1)}, bf16[8,4,160,128]{3,2,1,0:T(8,128)(2,1)S(1)}, bf16[32,128,128]{2,1,0:T(8,128)(2,1)S(1)}) %tuple.22), branch_computations={%region_0.1_spmd, %region_1.2_spmd} | conditional | bytes 9437248 | solution.py:275
  23.2 0.6 arrange.2
  23.8 33.3 %all_to_all.18.first.second = bf16[16,1,4,16,128]{4,3,2,1,0:T(8,128)(2,1)S(1)} all-to-all(bf16[16,1,4,16,128]{4,3,2,1,0:T(8,128)(2,1)S(1)} %arrange.2), channel_id=1, replica_groups=mesh['zh'=4,'zl'=4,'x'=4,'c'=2,'ta'=4] {'zh','zl'}, dimensions={0} | all-to-all | bytes 524288 | tf_op jit(solution)/shard_map/cond/branch_0_fun/all_to_all | solution.py:260
  57.2 1.3 %products.2 = f32[32,2,8,128]{3,2,1,0:T(8,128)} custom-call(s32[8]{0:T(128)S(1)} %get-tuple-element.20.meta, bf16[16,1,4,16,128]{4,3,2,1,0:T(8,128)(2,1)S(1)} %all_to_all.18.first.second, bf16[16,1,4,16,128]{4,3,2,1,0:T(8,128)(2,1)S(1)} %all_to_all.18.first.second, bf16[32,128,128]{2,1,0:T(8,128)(2,1)S(1)} %get-tuple-element.22.ref), custom_call_target="tpu_custom_call" | custom-call | tf_op jit(solution)/shard_map/cond/branch_0_fun/products/pallas_call | solution.py:71
  58.5 5.3 %all-to-all-start.3 = ((f32[32,2,8,128]{3,2,1,0:T(8,128)}), f32[32,2,8,128]{3,2,1,0:T(8,128)S(1)}, u32[]{:S(2)}, u32[]{:S(2)}) async-start(f32[32,2,8,128]{3,2,1,0:T(8,128)} %get-tuple-element.38), calls=%async_computation.3 | async-start | bytes 524288 | tf_op jit(solution)/shard_map/all_to_all | solution.py:280
  63.8 0.0 copy-done.4
  63.8 0.1 copy.10
  63.9 0.6 reshape.6.filt
  64.5 0.0 copy-done.3
  64.5 0.8 copy.11.taps
  65.4 2.3 %weigh.1.weights = bf16[256,256]{1,0:T(8,128)(2,1)S(1)} custom-call(s32[8]{0:T(128)S(1)} %stack.19.meta, s32[2,256]{1,0:T(2,128)} %offsets.1, s32[2,256]{1,0:T(2,128)} %bands.1, f32[2,256,4]{2,1,0:T(8,128)} %copy.11.taps), custom_call_target="tpu_custom_call" | custom-call | tf_op jit(solution)/shard_map/weigh/pallas_call | solution.py:118
  67.7 7.3 %all-to-all-done.3.pieces = f32[32,2,8,128]{3,2,1,0:T(8,128)S(1)} async-done(((f32[32,2,8,128]{3,2,1,0:T(8,128)}), f32[32,2,8,128]{3,2,1,0:T(8,128)S(1)}, u32[]{:S(2)}, u32[]{:S(2)}) %all-to-all-start.3) | async-done | bytes 262176 | tf_op jit(solution)/shard_map/all_to_all | solution.py:280
  74.9 1.1 %brink.1 = (f32[1,256]{1,0:T(1,128)S(1)}, f32[1,256]{1,0:T(1,128)S(1)}) custom-call(f32[72]{0:T(128)} %reshape.6.filt, bf16[256,256]{1,0:T(8,128)(2,1)S(1)} %weigh.1.weights, f32[32,2,8,128]{3,2,1,0:T(8,128)S(1)} %all-to-all-done.3.pieces), custom_call_target="tpu_custom_call" | custom-call | tf_op jit(solution)/shard_map/brink/pallas_call | solution.py:168
  76.0 3.5 %collective-permute-start = (f32[1,256]{1,0:T(1,128)S(1)}, f32[1,256]{1,0:T(1,128)S(1)}, u32[]{:S(2)}, u32[]{:S(2)}) collective-permute-start(f32[1,256]{1,0:T(1,128)S(1)} %get-tuple-element.28), channel_id=1, source_target_pairs={{0,1},{1,2},{2,3},{4,5},{5,6},{6,7},{8,9},{9,10},{10,11},{12,13},{... | collective-permute-start | bytes 3080 | tf_op jit(solution)/shard_map/ppermute | solution.py:286
  79.5 2.4 %collective-permute-start.1 = (f32[1,256]{1,0:T(1,128)S(1)}, f32[1,256]{1,0:T(1,128)S(1)}, u32[]{:S(2)}, u32[]{:S(2)}) collective-permute-start(f32[1,256]{1,0:T(1,128)S(1)} %get-tuple-element.29), channel_id=1, source_target_pairs={{1,0},{2,1},{3,2},{5,4},{6,5},{7,6},{9,8},{10,9},{11,10},{13,12},{... | collective-permute-start | bytes 3080 | tf_op jit(solution)/shard_map/ppermute | solution.py:287
  81.9 2.0 %filtered.1.cost = f32[256,128]{1,0:T(8,128)S(1)} custom-call(f32[72]{0:T(128)} %reshape.6.filt, bf16[256,256]{1,0:T(8,128)(2,1)S(1)} %weigh.1.weights, f32[32,2,8,128]{3,2,1,0:T(8,128)S(1)} %all-to-all-done.3.pieces), custom_call_target="tpu_custom_call" | custom-call | tf_op jit(solution)/shard_map/filtered/pallas_call | solution.py:223
  83.9 0.0 collective-permute-done.from_left
  83.9 1.1 %collective-permute-done.1.from_right = f32[1,256]{1,0:T(1,128)S(1)} collective-permute-done((f32[1,256]{1,0:T(1,128)S(1)}, f32[1,256]{1,0:T(1,128)S(1)}, u32[]{:S(2)}, u32[]{:S(2)}) %collective-permute-start.1) | collective-permute-done | bytes 1056 | tf_op jit(solution)/shard_map/ppermute | solution.py:287
  85.0 0.7 expected.1
  (1 shorter events, 0.0 us)
Async XLA Ops:
  0.0 4.4 %copy-start.5 = (s32[2]{0:T(128)S(1)}, s32[2]{0:T(128)}, u32[]{:S(2)}) copy-start(s32[2]{0:T(128)} %param.11) | copy-start | bytes 28
  0.0 23.2 %copy-start = (bf16[32,128,128]{2,1,0:T(8,128)(2,1)S(1)}, bf16[32,128,128]{2,1,0:T(8,128)(2,1)}, u32[]{:S(2)}) copy-start(bf16[32,128,128]{2,1,0:T(8,128)(2,1)} %param.9) | copy-start | bytes 3145732
  0.0 23.2 %all-to-all-start.2 = ((bf16[32,160,128]{2,1,0:T(8,128)(2,1)}), bf16[32,160,128]{2,1,0:T(8,128)(2,1)S(1)}, u32[]{:S(2)}, u32[]{:S(2)}) async-start(bf16[32,160,128]{2,1,0:T(8,128)(2,1)} %bitcast.12), calls=%async_computation.2 | async-start | bytes 2621440 | tf_op jit(solution)/shard_map/all_to_all | solution.py:272
  23.2 40.6 %copy-start.4 = (f32[8,3,3]{0,2,1:T(4,128)S(1)}, f32[8,3,3]{0,2,1:T(4,128)}, u32[]{:S(2)}) copy-start(f32[8,3,3]{0,2,1:T(4,128)} %param.15) | copy-start | bytes 868
  23.2 41.3 %copy-start.3 = (f32[2,256,4]{1,2,0:T(4,128)S(1)}, f32[2,256,4]{1,2,0:T(4,128)}, u32[]{:S(2)}) copy-start(f32[2,256,4]{1,2,0:T(4,128)} %param.14) | copy-start | bytes 24580
  58.5 16.4 %all-to-all-start.3 = ((f32[32,2,8,128]{3,2,1,0:T(8,128)}), f32[32,2,8,128]{3,2,1,0:T(8,128)S(1)}, u32[]{:S(2)}, u32[]{:S(2)}) async-start(f32[32,2,8,128]{3,2,1,0:T(8,128)} %get-tuple-element.38), calls=%async_computation.3 | async-start | bytes 524288 | tf_op jit(solution)/shard_map/all_to_all | solution.py:280
  76.0 7.8 %collective-permute-start = (f32[1,256]{1,0:T(1,128)S(1)}, f32[1,256]{1,0:T(1,128)S(1)}, u32[]{:S(2)}, u32[]{:S(2)}) collective-permute-start(f32[1,256]{1,0:T(1,128)S(1)} %get-tuple-element.28), channel_id=1, source_target_pairs={{0,1},{1,2},{2,3},{4,5},{5,6},{6,7},{8,9},{9,10},{10,11},{12,13},{... | collective-permute-start | bytes 3080 | tf_op jit(solution)/shard_map/ppermute | solution.py:286
  79.5 5.5 %collective-permute-start.1 = (f32[1,256]{1,0:T(1,128)S(1)}, f32[1,256]{1,0:T(1,128)S(1)}, u32[]{:S(2)}, u32[]{:S(2)}) collective-permute-start(f32[1,256]{1,0:T(1,128)S(1)} %get-tuple-element.29), channel_id=1, source_target_pairs={{1,0},{2,1},{3,2},{5,4},{6,5},{7,6},{9,8},{10,9},{11,10},{13,12},{... | collective-permute-start | bytes 3080 | tf_op jit(solution)/shard_map/ppermute | solution.py:287

commit v5 on v4

--- a/solution.py
+++ b/solution.py
@@ -55,12 +55,14 @@
         refs[chan] = ref[chan].astype(jnp.float32)
     for row in range(SPAN):
         start = row // ZL + jnp.where(row % ZL > phase, 1, 0)
+        totals = []
         for view in range(2):
             total = jnp.zeros((8, 128), jnp.float32)
             for chan in range(CG):
                 line = refs[chan, row : row + 1, :]
                 total = total + line * rows[view, chan, pl.ds(start, 8), :]
-            out[row, view] = total
+            totals.append(total)
+        out[row] = jnp.concatenate(totals, axis=0)
 
 
 def products_call(meta, arrived, ref):
@@ -78,13 +80,13 @@
                 spec(1),
                 pl.BlockSpec((CG, SPAN, 128), lambda i, m: (m[6], m[4], 0)),
             ],
-            out_specs=pl.BlockSpec((SPAN, 2, 8, 128), lambda i, m: (0, 0, 0, 0)),
+            out_specs=pl.BlockSpec((SPAN, 16, 128), lambda i, m: (0, 0, 0)),
             scratch_shapes=[
                 pltpu.VMEM((2, CG, 16, 128), jnp.float32),
                 pltpu.VMEM((CG, SPAN, 128), jnp.float32),
             ],
         ),
-        out_shape=pltpu.VMEM((SPAN, 2, 8, 128), jnp.float32),
+        out_shape=pltpu.VMEM((SPAN, 16, 128), jnp.float32),
         name="products",
     )(meta, arrived, arrived, ref)
 
@@ -137,7 +139,7 @@
     for block in range(ZL):
         ends = jnp.zeros((16, 128), jnp.float32)
         for group in range(G):
-            piece = pieces[block * G + group].reshape(16, 128)
+            piece = pieces[block * G + group]
             ends = jnp.where(lane == group, pltpu.roll(piece, group + 1, 1), ends)
             ends = jnp.where(lane == G + group, pltpu.roll(piece, G + group, 1), ends)
         high = ends.astype(jnp.bfloat16)
@@ -182,7 +184,7 @@
     for group in range(G):
         lanes = slice(128 * group, 128 * group + 128)
         for block in range(ZL):
-            piece = pieces[block * G + group].reshape(16, 128)
+            piece = pieces[block * G + group]
             high = piece.astype(jnp.bfloat16)
             low = (piece - high.astype(jnp.float32)).astype(jnp.bfloat16)
             for copy in range(2):
@@ -273,11 +275,12 @@
     weights = weigh_call(meta, offsets, bands, taps)
     arrived = near_core(arrived.reshape(G, CG, 160, 128))
     pieces = lax.cond(
-        far[0] == far[1],
+        jnp.logical_and(far[0] == far[1], near[0] != near[1]),
         lambda: spread(meta, arrived, ref_feats, (0, 1)),
         lambda: spread(meta, arrived, ref_feats, (7,)),
     )
-    pieces = lax.all_to_all(pieces, ("zl", "x", "c"), 0, 0, tiled=True)
+    pieces = lax.all_to_all(pieces.astype(jnp.float16), ("zl", "x", "c"), 0, 0, tiled=True)
+    pieces = pieces.astype(jnp.float32)
     filt = filt.reshape(G * 9)
     weights = near_core(weights)
     pieces = near_core(pieces)

time: 86.1 us -> 83.7 us (0.972)
  waiting for transfers between devices: 23.2 us -> 19.5 us
  between operations: 3.27 us -> 4.52 us
    all_to_all x1, waiting for transfers between devices: 7.25 us -> 4.84 us  [body(): lax.all_to_all(pieces.astype(jnp.float16), ('zl', 'x', 'c'), 0, 0, tiled=...]
    all_to_all x1, waiting for transfers between devices: 14.8 us -> 13.6 us  [body(): arrived = lax.all_to_all(crops[0], ('x', 'c'), 0, 0, tiled=True)]
where the time goes in v5:
time: 83.7 us; the launch traced here: 83.3 us
  blocking collectives  33.3 us (40%)
  waiting for transfers between devices  19.5 us (23%)
  starting transfers between devices  15.6 us (19%)
  Pallas kernels  7.26 us (9%)
  between operations  4.52 us (5%)
  local copies, waits for them, and re-layouts  2.34 us (3%)
    all_to_all x1, blocking collectives, spread(): windows = lax.all_to_all(windows, ('zh', 'zl'), 0, 0, tiled=True)  33.3 us
    all_to_all x1, waiting for transfers between devices, body(): arrived = lax.all_to_all(crops[0], ('x', 'c'), 0, 0, tiled=True)  13.6 us
    all_to_all x1, starting transfers between devices, body(): lax.all_to_all(pieces.astype(jnp.float16), ('zl', 'x', 'c'), 0, 0, tiled=...  5.31 us
    all_to_all x1, waiting for transfers between devices, body(): lax.all_to_all(pieces.astype(jnp.float16), ('zl', 'x', 'c'), 0, 0, tiled=...  4.84 us
    all_to_all x1, starting transfers between devices, body(): arrived = lax.all_to_all(crops[0], ('x', 'c'), 0, 0, tiled=True)  4.43 us
    ppermute x1, starting transfers between devices, body(): lax.ppermute(right, 'ta', [(i, i + 1) for i in range(count - 1)])  3.5 us
    ppermute x1, starting transfers between devices, body(): lax.ppermute(left, 'ta', [(i + 1, i) for i in range(count - 1)])  2.35 us
    pallas_call x1, Pallas kernels, weigh_call(): pl.pallas_call(weigh, grid_spec=pltpu.PrefetchScalarGridSpec(num_scalar_p...  2.27 us
  transfers between devices with their start and end apart: 4, of which 3 were waited for; matrix products, arithmetic and copies ran while one was open for 3% of the time, Pallas kernels for 5%

profile of v5, /device:TPU:8, one launch (start us, length us, event | category | flops | bytes accessed | tf_op | source)
XLA Modules:
  0.0 83.3 jit_solution(6390198799839810225)
XLA Ops:
  0.0 0.0 copy-start.3
  0.0 0.0 copy-start
  0.0 4.4 %all-to-all-start.2 = ((bf16[32,160,128]{2,1,0:T(8,128)(2,1)}), bf16[32,160,128]{2,1,0:T(8,128)(2,1)S(1)}, u32[]{:S(2)}, u32[]{:S(2)}) async-start(bf16[32,160,128]{2,1,0:T(8,128)(2,1)} %bitcast.12), calls=%async_computation.2 | async-start | bytes 2621440 | tf_op jit(solution)/shard_map/all_to_all | solution.py:274
  4.4 0.0 copy-done.3
  4.5 0.7 fusion
  9.6 0.1 stack.19.meta
  9.6 13.6 %all-to-all-done.2 = bf16[32,160,128]{2,1,0:T(8,128)(2,1)S(1)} async-done(((bf16[32,160,128]{2,1,0:T(8,128)(2,1)}), bf16[32,160,128]{2,1,0:T(8,128)(2,1)S(1)}, u32[]{:S(2)}, u32[]{:S(2)}) %all-to-all-start.2) | async-done | bytes 1310752 | tf_op jit(solution)/shard_map/all_to_all | solution.py:274
  23.2 0.0 copy-done
  23.2 0.0 copy-start.2
  23.2 0.0 copy-start.1
  23.2 34.6 %conditional.1 = (f32[32,16,128]{2,1,0:T(8,128)S(1)}) conditional(s32[]{:T(128)} %convert_element_type.9, (s32[8]{0:T(128)S(1)}, bf16[8,4,160,128]{3,2,1,0:T(8,128)(2,1)S(1)}, bf16[32,128,128]{2,1,0:T(8,128)(2,1)S(1)}) %tuple.21, (s32[8]{0:T(128)S(1)}, bf16[8,4,160,128]{3,2,1,0:T(8,128)(2,1)S(1)}, bf16[32,128,128]{2,1,0:T(8,128)(2,1)S(1)}) %tuple.22), branch_computations={%region_0.1_spmd, %region_1.2_spmd} | conditional | bytes 1048584 | solution.py:277
  23.2 0.6 arrange.2
  23.8 33.3 %all_to_all.18.first.second = bf16[16,1,4,16,128]{4,3,2,1,0:T(8,128)(2,1)S(1)} all-to-all(bf16[16,1,4,16,128]{4,3,2,1,0:T(8,128)(2,1)S(1)} %arrange.2), channel_id=1, replica_groups=mesh['zh'=4,'zl'=4,'x'=4,'c'=2,'ta'=4] {'zh','zl'}, dimensions={0} | all-to-all | bytes 524288 | tf_op jit(solution)/shard_map/cond/branch_0_fun/all_to_all | solution.py:262
  57.2 0.6 products.2
  57.8 0.7 convert_element_type.10
  58.5 5.3 %all-to-all-start.3 = ((f16[32,16,128]{2,1,0:T(8,128)(2,1)}), f16[32,16,128]{2,1,0:T(8,128)(2,1)S(1)}, u32[]{:S(2)}, u32[]{:S(2)}) async-start(f16[32,16,128]{2,1,0:T(8,128)(2,1)} %convert_element_type.10), calls=%async_computation.3 | async-start | bytes 262144 | tf_op jit(solution)/shard_map/all_to_all | solution.py:282
  63.8 0.0 copy-done.2
  63.8 0.1 copy.10
  63.9 0.6 reshape.6.filt
  64.5 0.0 copy-done.1
  64.5 0.9 %copy.11.taps = f32[2,256,4]{2,1,0:T(8,128)} copy(f32[2,256,4]{1,2,0:T(4,128)S(1)} %copy-done.1) | data formatting | bytes 16384 | tf_op args[5]
  65.4 2.3 %weigh.1.weights = bf16[256,256]{1,0:T(8,128)(2,1)S(1)} custom-call(s32[8]{0:T(128)S(1)} %stack.19.meta, s32[2,256]{1,0:T(2,128)} %offsets.1, s32[2,256]{1,0:T(2,128)} %bands.1, f32[2,256,4]{2,1,0:T(8,128)} %copy.11.taps), custom_call_target="tpu_custom_call" | custom-call | tf_op jit(solution)/shard_map/weigh/pallas_call | solution.py:120
  67.7 4.8 %all-to-all-done.3 = f16[32,16,128]{2,1,0:T(8,128)(2,1)S(1)} async-done(((f16[32,16,128]{2,1,0:T(8,128)(2,1)}), f16[32,16,128]{2,1,0:T(8,128)(2,1)S(1)}, u32[]{:S(2)}, u32[]{:S(2)}) %all-to-all-start.3) | async-done | bytes 131104 | tf_op jit(solution)/shard_map/all_to_all | solution.py:282
  72.5 1.1 %brink.1 = (f32[1,256]{1,0:T(1,128)S(1)}, f32[1,256]{1,0:T(1,128)S(1)}) custom-call(f32[72]{0:T(128)} %reshape.6.filt, bf16[256,256]{1,0:T(8,128)(2,1)S(1)} %weigh.1.weights, f32[32,16,128]{2,1,0:T(8,128)S(1)} %convert_element_type.11.pieces), custom_call_target="tpu_custom_call" | custom-call | tf_op jit(solution)/shard_map/brink/pallas_call | solution.py:170
  73.6 3.5 %collective-permute-start = (f32[1,256]{1,0:T(1,128)S(1)}, f32[1,256]{1,0:T(1,128)S(1)}, u32[]{:S(2)}, u32[]{:S(2)}) collective-permute-start(f32[1,256]{1,0:T(1,128)S(1)} %get-tuple-element.28), channel_id=1, source_target_pairs={{0,1},{1,2},{2,3},{4,5},{5,6},{6,7},{8,9},{9,10},{10,11},{12,13},{... | collective-permute-start | bytes 3080 | tf_op jit(solution)/shard_map/ppermute | solution.py:289
  77.2 2.4 %collective-permute-start.1 = (f32[1,256]{1,0:T(1,128)S(1)}, f32[1,256]{1,0:T(1,128)S(1)}, u32[]{:S(2)}, u32[]{:S(2)}) collective-permute-start(f32[1,256]{1,0:T(1,128)S(1)} %get-tuple-element.29), channel_id=1, source_target_pairs={{1,0},{2,1},{3,2},{5,4},{6,5},{7,6},{9,8},{10,9},{11,10},{13,12},{... | collective-permute-start | bytes 3080 | tf_op jit(solution)/shard_map/ppermute | solution.py:290
  79.5 2.0 %filtered.1.cost = f32[256,128]{1,0:T(8,128)S(1)} custom-call(f32[72]{0:T(128)} %reshape.6.filt, bf16[256,256]{1,0:T(8,128)(2,1)S(1)} %weigh.1.weights, f32[32,16,128]{2,1,0:T(8,128)S(1)} %convert_element_type.11.pieces), custom_call_target="tpu_custom_call" | custom-call | tf_op jit(solution)/shard_map/filtered/pallas_call | solution.py:225
  81.5 0.0 collective-permute-done.from_left
  81.5 1.1 %collective-permute-done.1.from_right = f32[1,256]{1,0:T(1,128)S(1)} collective-permute-done((f32[1,256]{1,0:T(1,128)S(1)}, f32[1,256]{1,0:T(1,128)S(1)}, u32[]{:S(2)}, u32[]{:S(2)}) %collective-permute-start.1) | collective-permute-done | bytes 1056 | tf_op jit(solution)/shard_map/ppermute | solution.py:290
  82.6 0.7 expected.1
  (2 shorter events, 0.0 us)
Async XLA Ops:
  0.0 4.4 %copy-start.3 = (s32[2]{0:T(128)S(1)}, s32[2]{0:T(128)}, u32[]{:S(2)}) copy-start(s32[2]{0:T(128)} %param.11) | copy-start | bytes 28
  0.0 23.2 %copy-start = (bf16[32,128,128]{2,1,0:T(8,128)(2,1)S(1)}, bf16[32,128,128]{2,1,0:T(8,128)(2,1)}, u32[]{:S(2)}) copy-start(bf16[32,128,128]{2,1,0:T(8,128)(2,1)} %param.9) | copy-start | bytes 3145732
  0.0 23.2 %all-to-all-start.2 = ((bf16[32,160,128]{2,1,0:T(8,128)(2,1)}), bf16[32,160,128]{2,1,0:T(8,128)(2,1)S(1)}, u32[]{:S(2)}, u32[]{:S(2)}) async-start(bf16[32,160,128]{2,1,0:T(8,128)(2,1)} %bitcast.12), calls=%async_computation.2 | async-start | bytes 2621440 | tf_op jit(solution)/shard_map/all_to_all | solution.py:274
  23.2 40.6 %copy-start.2 = (f32[8,3,3]{0,2,1:T(4,128)S(1)}, f32[8,3,3]{0,2,1:T(4,128)}, u32[]{:S(2)}) copy-start(f32[8,3,3]{0,2,1:T(4,128)} %param.15) | copy-start | bytes 868
  23.2 41.3 %copy-start.1 = (f32[2,256,4]{1,2,0:T(4,128)S(1)}, f32[2,256,4]{1,2,0:T(4,128)}, u32[]{:S(2)}) copy-start(f32[2,256,4]{1,2,0:T(4,128)} %param.14) | copy-start | bytes 24580
  58.5 14.0 %all-to-all-start.3 = ((f16[32,16,128]{2,1,0:T(8,128)(2,1)}), f16[32,16,128]{2,1,0:T(8,128)(2,1)S(1)}, u32[]{:S(2)}, u32[]{:S(2)}) async-start(f16[32,16,128]{2,1,0:T(8,128)(2,1)} %convert_element_type.10), calls=%async_computation.3 | async-start | bytes 262144 | tf_op jit(solution)/shard_map/all_to_all | solution.py:282
  73.6 7.8 %collective-permute-start = (f32[1,256]{1,0:T(1,128)S(1)}, f32[1,256]{1,0:T(1,128)S(1)}, u32[]{:S(2)}, u32[]{:S(2)}) collective-permute-start(f32[1,256]{1,0:T(1,128)S(1)} %get-tuple-element.28), channel_id=1, source_target_pairs={{0,1},{1,2},{2,3},{4,5},{5,6},{6,7},{8,9},{9,10},{10,11},{12,13},{... | collective-permute-start | bytes 3080 | tf_op jit(solution)/shard_map/ppermute | solution.py:289
  77.2 5.5 %collective-permute-start.1 = (f32[1,256]{1,0:T(1,128)S(1)}, f32[1,256]{1,0:T(1,128)S(1)}, u32[]{:S(2)}, u32[]{:S(2)}) collective-permute-start(f32[1,256]{1,0:T(1,128)S(1)} %get-tuple-element.29), channel_id=1, source_target_pairs={{1,0},{2,1},{3,2},{5,4},{6,5},{7,6},{9,8},{10,9},{11,10},{13,12},{... | collective-permute-start | bytes 3080 | tf_op jit(solution)/shard_map/ppermute | solution.py:290

commit v6 on v5

--- a/solution.py
+++ b/solution.py
@@ -260,7 +260,7 @@
 def spread(meta, arrived, ref_feats, picks):
     windows = arrange_call(meta, arrived, picks)
     windows = lax.all_to_all(windows, ("zh", "zl"), 0, 0, tiled=True)
-    return products_call(meta, near_core(windows), ref_feats)
+    return products_call(meta, near_core(windows), ref_feats).astype(jnp.float16)
 
 
 def body(ref_feats, crops, owner, offsets, bands, taps, filt):
@@ -273,15 +273,16 @@
     meta = jnp.stack([near[0], near[1], far[0], far[1], block, phase, group, mine]).astype(jnp.int32)
     arrived = lax.all_to_all(crops[0], ("x", "c"), 0, 0, tiled=True)
     weights = weigh_call(meta, offsets, bands, taps)
+    filt = filt.reshape(G * 9)
+    meta, weights, filt = lax.optimization_barrier((meta, weights, filt))
     arrived = near_core(arrived.reshape(G, CG, 160, 128))
     pieces = lax.cond(
         jnp.logical_and(far[0] == far[1], near[0] != near[1]),
         lambda: spread(meta, arrived, ref_feats, (0, 1)),
         lambda: spread(meta, arrived, ref_feats, (7,)),
     )
-    pieces = lax.all_to_all(pieces.astype(jnp.float16), ("zl", "x", "c"), 0, 0, tiled=True)
+    pieces = lax.all_to_all(pieces, ("zl", "x", "c"), 0, 0, tiled=True)
     pieces = pieces.astype(jnp.float32)
-    filt = filt.reshape(G * 9)
     weights = near_core(weights)
     pieces = near_core(pieces)
     right, left = brink_call(filt, weights, pieces)

time: 83.7 us -> 82.8 us (0.989)
  blocking collectives: 33.3 us -> 47.1 us
  waiting for transfers between devices: 19.5 us -> 11 us
  starting transfers between devices: 15.6 us -> 10.3 us
    all_to_all x0 -> x1, blocking collectives: none -> 13.8 us  [body(): pieces = lax.all_to_all(pieces, ('zl', 'x', 'c'), 0, 0, tiled=True)]
    all_to_all x1 -> x0, starting transfers between devices: 5.31 us -> none  [body(): lax.all_to_all(pieces.astype(jnp.float16), ('zl', 'x', 'c'), 0, 0, tiled=...]
    all_to_all x1 -> x0, waiting for transfers between devices: 4.84 us -> none  [body(): lax.all_to_all(pieces.astype(jnp.float16), ('zl', 'x', 'c'), 0, 0, tiled=...]
    all_to_all x1, waiting for transfers between devices: 13.6 us -> 9.91 us  [body(): arrived = lax.all_to_all(crops[0], ('x', 'c'), 0, 0, tiled=True)]
  transfers between devices with their start and end apart: 4 -> 3, of which waited for: 3 -> 2; matrix products, arithmetic and copies ran while one was open for 3% -> 3% of each run, Pallas kernels for 5% -> 5%
where the time goes in v6:
time: 82.8 us; the launch traced here: 82.5 us
  blocking collectives  47.1 us (57%)
  waiting for transfers between devices  11 us (13%)
  starting transfers between devices  10.3 us (12%)
  Pallas kernels  7.26 us (9%)
  between operations  4.37 us (5%)
  local copies, waits for them, and re-layouts  2.29 us (3%)
    all_to_all x1, blocking collectives, spread(): windows = lax.all_to_all(windows, ('zh', 'zl'), 0, 0, tiled=True)  33.3 us
    all_to_all x1, blocking collectives, body(): pieces = lax.all_to_all(pieces, ('zl', 'x', 'c'), 0, 0, tiled=True)  13.8 us
    all_to_all x1, waiting for transfers between devices, body(): arrived = lax.all_to_all(crops[0], ('x', 'c'), 0, 0, tiled=True)  9.91 us
    all_to_all x1, starting transfers between devices, body(): arrived = lax.all_to_all(crops[0], ('x', 'c'), 0, 0, tiled=True)  4.44 us
    ppermute x1, starting transfers between devices, body(): lax.ppermute(right, 'ta', [(i, i + 1) for i in range(count - 1)])  3.49 us
    ppermute x1, starting transfers between devices, body(): lax.ppermute(left, 'ta', [(i + 1, i) for i in range(count - 1)])  2.36 us
    pallas_call x1, Pallas kernels, weigh_call(): pl.pallas_call(weigh, grid_spec=pltpu.PrefetchScalarGridSpec(num_scalar_p...  2.27 us
    pallas_call x1, Pallas kernels, filtered_call(): pl.pallas_call(filtered, in_specs=[pl.BlockSpec(memory_space=pltpu.SMEM),...  1.95 us
  transfers between devices with their start and end apart: 3, of which 2 were waited for; matrix products, arithmetic and copies ran while one was open for 3% of the time, Pallas kernels for 5%

profile of v6, /device:TPU:8, one launch (start us, length us, event | category | flops | bytes accessed | tf_op | source)
XLA Modules:
  0.0 82.5 jit_solution(9513776811466897972)
XLA Ops:
  0.0 0.0 copy-start.3
  0.0 0.0 copy-start.2
  0.0 0.0 copy-start.1
  0.0 0.0 copy-start
  0.0 4.4 %all-to-all-start.2 = ((bf16[32,160,128]{2,1,0:T(8,128)(2,1)}), bf16[32,160,128]{2,1,0:T(8,128)(2,1)S(1)}, u32[]{:S(2)}, u32[]{:S(2)}) async-start(bf16[32,160,128]{2,1,0:T(8,128)(2,1)} %bitcast.12), calls=%async_computation.2 | async-start | bytes 2621440 | tf_op jit(solution)/shard_map/all_to_all | solution.py:274
  4.5 0.0 copy-done.3
  4.5 0.6 fusion
  9.4 0.0 copy-done.2
  9.4 0.1 copy.11
  9.5 0.6 reshape.6.filt
  10.1 0.0 copy-done.1
  10.1 0.9 %copy.10.taps = f32[2,256,4]{2,1,0:T(8,128)} copy(f32[2,256,4]{1,2,0:T(4,128)S(1)} %copy-done.1) | data formatting | bytes 16384 | tf_op args[5]
  11.0 0.1 stack.19.meta
  11.1 2.3 %weigh.1.weights = bf16[256,256]{1,0:T(8,128)(2,1)S(1)} custom-call(s32[8]{0:T(128)S(1)} %stack.19.meta, s32[2,256]{1,0:T(2,128)} %offsets.1, s32[2,256]{1,0:T(2,128)} %bands.1, f32[2,256,4]{2,1,0:T(8,128)} %copy.10.taps), custom_call_target="tpu_custom_call" | custom-call | tf_op jit(solution)/shard_map/weigh/pallas_call | solution.py:120
  13.3 9.9 %all-to-all-done.2 = bf16[32,160,128]{2,1,0:T(8,128)(2,1)S(1)} async-done(((bf16[32,160,128]{2,1,0:T(8,128)(2,1)}), bf16[32,160,128]{2,1,0:T(8,128)(2,1)S(1)}, u32[]{:S(2)}, u32[]{:S(2)}) %all-to-all-start.2) | async-done | bytes 1310752 | tf_op jit(solution)/shard_map/all_to_all | solution.py:274
  23.2 0.0 copy-done
  23.2 34.6 %conditional.2 = (f32[32,16,128]{2,1,0:T(8,128)S(1)}) conditional(s32[]{:T(128)} %convert_element_type.11, (s32[8]{0:T(128)S(1)}, bf16[8,4,160,128]{3,2,1,0:T(8,128)(2,1)S(1)}, bf16[32,128,128]{2,1,0:T(8,128)(2,1)S(1)}) %tuple.26, (s32[8]{0:T(128)S(1)}, bf16[8,4,160,128]{3,2,1,0:T(8,128)(2,1)S(1)}, bf16[32,128,128]{2,1,0:T(8,128)(2,1)S(1)}) %tuple.27), branch_computations={%region_0.1_spmd, %region_1.2_spmd} | conditional | bytes 1048584
  23.2 0.6 arrange.2
  23.8 33.3 %all_to_all.18.first.second = bf16[16,1,4,16,128]{4,3,2,1,0:T(8,128)(2,1)S(1)} all-to-all(bf16[16,1,4,16,128]{4,3,2,1,0:T(8,128)(2,1)S(1)} %arrange.2), channel_id=1, replica_groups=mesh['zh'=4,'zl'=4,'x'=4,'c'=2,'ta'=4] {'zh','zl'}, dimensions={0} | all-to-all | bytes 524288 | tf_op jit(solution)/shard_map/cond/branch_0_fun/all_to_all | solution.py:262
  57.2 0.6 products.2
  57.9 13.8 %all_to_all.20 = f16[32,16,128]{2,1,0:T(8,128)(2,1)S(1)} all-to-all(f16[32,16,128]{2,1,0:T(8,128)(2,1)S(1)} %convert_element_type.12), channel_id=1, replica_groups=mesh['zh'=4,'zl'=4,'x'=4,'c'=2,'ta'=4] {'zl','x','c'}, dimensions={0} | all-to-all | bytes 262144 | tf_op jit(solution)/shard_map/all_to_all | solution.py:284
  71.7 1.1 %brink.1 = (f32[1,256]{1,0:T(1,128)S(1)}, f32[1,256]{1,0:T(1,128)S(1)}) custom-call(f32[72]{0:T(128)} %reshape.6.filt, bf16[256,256]{1,0:T(8,128)(2,1)S(1)} %weigh.1.weights, f32[32,16,128]{2,1,0:T(8,128)S(1)} %convert_element_type.13.pieces), custom_call_target="tpu_custom_call" | custom-call | tf_op jit(solution)/shard_map/brink/pallas_call | solution.py:170
  72.8 3.5 %collective-permute-start = (f32[1,256]{1,0:T(1,128)S(1)}, f32[1,256]{1,0:T(1,128)S(1)}, u32[]{:S(2)}, u32[]{:S(2)}) collective-permute-start(f32[1,256]{1,0:T(1,128)S(1)} %get-tuple-element.36), channel_id=1, source_target_pairs={{0,1},{1,2},{2,3},{4,5},{5,6},{6,7},{8,9},{9,10},{10,11},{12,13},{... | collective-permute-start | bytes 3080 | tf_op jit(solution)/shard_map/ppermute | solution.py:290
  76.3 2.4 %collective-permute-start.1 = (f32[1,256]{1,0:T(1,128)S(1)}, f32[1,256]{1,0:T(1,128)S(1)}, u32[]{:S(2)}, u32[]{:S(2)}) collective-permute-start(f32[1,256]{1,0:T(1,128)S(1)} %get-tuple-element.37), channel_id=1, source_target_pairs={{1,0},{2,1},{3,2},{5,4},{6,5},{7,6},{9,8},{10,9},{11,10},{13,12},{... | collective-permute-start | bytes 3080 | tf_op jit(solution)/shard_map/ppermute | solution.py:291
  78.7 2.0 %filtered.1.cost = f32[256,128]{1,0:T(8,128)S(1)} custom-call(f32[72]{0:T(128)} %reshape.6.filt, bf16[256,256]{1,0:T(8,128)(2,1)S(1)} %weigh.1.weights, f32[32,16,128]{2,1,0:T(8,128)S(1)} %convert_element_type.13.pieces), custom_call_target="tpu_custom_call" | custom-call | tf_op jit(solution)/shard_map/filtered/pallas_call | solution.py:225
  80.6 0.0 collective-permute-done.from_left
  80.6 1.1 %collective-permute-done.1.from_right = f32[1,256]{1,0:T(1,128)S(1)} collective-permute-done((f32[1,256]{1,0:T(1,128)S(1)}, f32[1,256]{1,0:T(1,128)S(1)}, u32[]{:S(2)}, u32[]{:S(2)}) %collective-permute-start.1) | collective-permute-done | bytes 1056 | tf_op jit(solution)/shard_map/ppermute | solution.py:291
  81.8 0.7 expected.1
  (3 shorter events, 0.1 us)
Async XLA Ops:
  0.0 4.5 %copy-start.3 = (s32[2]{0:T(128)S(1)}, s32[2]{0:T(128)}, u32[]{:S(2)}) copy-start(s32[2]{0:T(128)} %param.11) | copy-start | bytes 28
  0.0 9.4 %copy-start.2 = (f32[8,3,3]{0,2,1:T(4,128)S(1)}, f32[8,3,3]{0,2,1:T(4,128)}, u32[]{:S(2)}) copy-start(f32[8,3,3]{0,2,1:T(4,128)} %param.15) | copy-start | bytes 868
  0.0 10.1 %copy-start.1 = (f32[2,256,4]{1,2,0:T(4,128)S(1)}, f32[2,256,4]{1,2,0:T(4,128)}, u32[]{:S(2)}) copy-start(f32[2,256,4]{1,2,0:T(4,128)} %param.14) | copy-start | bytes 24580
  0.0 23.2 %copy-start = (bf16[32,128,128]{2,1,0:T(8,128)(2,1)S(1)}, bf16[32,128,128]{2,1,0:T(8,128)(2,1)}, u32[]{:S(2)}) copy-start(bf16[32,128,128]{2,1,0:T(8,128)(2,1)} %param.9) | copy-start | bytes 3145732
  0.0 23.2 %all-to-all-start.2 = ((bf16[32,160,128]{2,1,0:T(8,128)(2,1)}), bf16[32,160,128]{2,1,0:T(8,128)(2,1)S(1)}, u32[]{:S(2)}, u32[]{:S(2)}) async-start(bf16[32,160,128]{2,1,0:T(8,128)(2,1)} %bitcast.12), calls=%async_computation.2 | async-start | bytes 2621440 | tf_op jit(solution)/shard_map/all_to_all | solution.py:274
  72.8 7.8 %collective-permute-start = (f32[1,256]{1,0:T(1,128)S(1)}, f32[1,256]{1,0:T(1,128)S(1)}, u32[]{:S(2)}, u32[]{:S(2)}) collective-permute-start(f32[1,256]{1,0:T(1,128)S(1)} %get-tuple-element.36), channel_id=1, source_target_pairs={{0,1},{1,2},{2,3},{4,5},{5,6},{6,7},{8,9},{9,10},{10,11},{12,13},{... | collective-permute-start | bytes 3080 | tf_op jit(solution)/shard_map/ppermute | solution.py:290
  76.3 5.5 %collective-permute-start.1 = (f32[1,256]{1,0:T(1,128)S(1)}, f32[1,256]{1,0:T(1,128)S(1)}, u32[]{:S(2)}, u32[]{:S(2)}) collective-permute-start(f32[1,256]{1,0:T(1,128)S(1)} %get-tuple-element.37), channel_id=1, source_target_pairs={{1,0},{2,1},{3,2},{5,4},{6,5},{7,6},{9,8},{10,9},{11,10},{13,12},{... | collective-permute-start | bytes 3080 | tf_op jit(solution)/shard_map/ppermute | solution.py:291

commit v7 on v6

--- a/solution.py
+++ b/solution.py
@@ -91,7 +91,15 @@
     )(meta, arrived, arrived, ref)
 
 
-def weigh(meta, offsets, bands, taps, out):
+def weigh(meta, filt, offsets, bands, taps, out, lines):
+    slot = lax.broadcasted_iota(jnp.int32, (8, 128), 1)
+    lag = lax.broadcasted_iota(jnp.int32, (8, 128), 0)
+    rows = jnp.zeros((8, 128), jnp.float32)
+    for i in range(3):
+        for group in range(G):
+            rows = jnp.where((lag == i) & (slot == group), filt[group * 9 + i * 3], rows)
+            rows = jnp.where((lag == i) & (slot == G + group), filt[group * 9 + i * 3 + 2], rows)
+    lines[...] = rows
     sub = lax.broadcasted_iota(jnp.int32, (128, D), 0)
     packed = jnp.zeros((128, D), jnp.float32)
     for view in range(2):
@@ -116,25 +124,25 @@
     out[:, 128:] = (total - high.astype(jnp.float32)).astype(jnp.bfloat16)
 
 
-def weigh_call(meta, offsets, bands, taps):
+def weigh_call(meta, filt, offsets, bands, taps):
     return pl.pallas_call(
         weigh,
         grid_spec=pltpu.PrefetchScalarGridSpec(
-            num_scalar_prefetch=1,
+            num_scalar_prefetch=2,
             grid=(1,),
             in_specs=[
-                pl.BlockSpec((2, D), lambda i, m: (0, 0)),
-                pl.BlockSpec((2, D), lambda i, m: (0, 0)),
-                pl.BlockSpec((2, D, 4), lambda i, m: (0, 0, 0)),
+                pl.BlockSpec((2, D), lambda i, m, f: (0, 0)),
+                pl.BlockSpec((2, D), lambda i, m, f: (0, 0)),
+                pl.BlockSpec((2, D, 4), lambda i, m, f: (0, 0, 0)),
             ],
-            out_specs=pl.BlockSpec((D, 256), lambda i, m: (0, 0)),
+            out_specs=[pl.BlockSpec((D, 256), lambda i, m, f: (0, 0)), pl.BlockSpec((8, 128), lambda i, m, f: (0, 0))],
         ),
-        out_shape=pltpu.VMEM((D, 256), jnp.bfloat16),
+        out_shape=[pltpu.VMEM((D, 256), jnp.bfloat16), pltpu.VMEM((8, 128), jnp.float32)],
         name="weigh",
-    )(meta, offsets, bands, taps)
-
-
-def brink(filt, weights, pieces, right, left, stack, sums):
+    )(meta, filt, offsets, bands, taps)
+
+
+def brink(lines, weights, pieces, right, left, stack, sums):
     lane = lax.broadcasted_iota(jnp.int32, (16, 128), 1)
     for block in range(ZL):
         ends = jnp.zeros((16, 128), jnp.float32)
@@ -150,13 +158,9 @@
             stack[at + 64 : at + 80, :] = low
     part = jnp.dot(weights[...], stack[...], preferred_element_type=jnp.float32) * 0.125
     part = part.astype(jnp.bfloat16).astype(jnp.float32)
-    slot = lax.broadcasted_iota(jnp.int32, (1, 128), 1)
     zero = jnp.zeros((8, 128), jnp.float32)
     for i in range(3):
-        line = jnp.zeros((1, 128), jnp.float32)
-        for group in range(G):
-            line = jnp.where(slot == group, filt[group * 9 + i * 3], line)
-            line = jnp.where(slot == G + group, filt[group * 9 + i * 3 + 2], line)
+        line = lines[i : i + 1, :]
         sums[i, 0:8, :] = zero
         sums[i, D + 8 : D + 16, :] = zero
         sums[i, 8 : D + 8, :] = part * line
@@ -165,19 +169,19 @@
     left[...] = jnp.sum(total[G : 2 * G], axis=0, keepdims=True)
 
 
-def brink_call(filt, weights, pieces):
+def brink_call(lines, weights, pieces):
     edge = pltpu.VMEM((1, D), jnp.float32)
     return pl.pallas_call(
         brink,
         in_specs=[
-            pl.BlockSpec(memory_space=pltpu.SMEM),
+            pl.BlockSpec(memory_space=pltpu.VMEM),
             pl.BlockSpec(memory_space=pltpu.VMEM),
             pl.BlockSpec(memory_space=pltpu.VMEM),
         ],
         out_shape=[edge, edge],
         scratch_shapes=[pltpu.VMEM((256, 128), jnp.bfloat16), pltpu.VMEM((3, D + 16, 128), jnp.float32)],
         name="brink",
-    )(filt, weights, pieces)
+    )(lines, weights, pieces)
 
 
 def filtered(filt, weights, pieces, cost, stack, volume, sums):
@@ -272,9 +276,9 @@
     mine = jnp.where(far[1] == block * ZL + phase, near[1], near[0])
     meta = jnp.stack([near[0], near[1], far[0], far[1], block, phase, group, mine]).astype(jnp.int32)
     arrived = lax.all_to_all(crops[0], ("x", "c"), 0, 0, tiled=True)
-    weights = weigh_call(meta, offsets, bands, taps)
     filt = filt.reshape(G * 9)
-    meta, weights, filt = lax.optimization_barrier((meta, weights, filt))
+    weights, lines = weigh_call(meta, filt, offsets, bands, taps)
+    meta, weights, lines, filt = lax.optimization_barrier((meta, weights, lines, filt))
     arrived = near_core(arrived.reshape(G, CG, 160, 128))
     pieces = lax.cond(
         jnp.logical_and(far[0] == far[1], near[0] != near[1]),
@@ -285,7 +289,7 @@
     pieces = pieces.astype(jnp.float32)
     weights = near_core(weights)
     pieces = near_core(pieces)
-    right, left = brink_call(filt, weights, pieces)
+    right, left = brink_call(near_core(lines), weights, pieces)
     count = lax.axis_size("ta")
     from_left = lax.ppermute(right, "ta", [(i, i + 1) for i in range(count - 1)])
     from_right = lax.ppermute(left, "ta", [(i + 1, i) for i in range(count - 1)])

time: 82.8 us -> 82.2 us (level)
  no operation moved by 1% of the time
where the time goes in v7:
time: 82.2 us; the launch traced here: 81.8 us
  blocking collectives  47.1 us (57%)
  waiting for transfers between devices  10.7 us (13%)
  starting transfers between devices  10.3 us (13%)
  Pallas kernels  6.74 us (8%)
  between operations  4.52 us (5%)
  local copies, waits for them, and re-layouts  2.33 us (3%)
    all_to_all x1, blocking collectives, spread(): windows = lax.all_to_all(windows, ('zh', 'zl'), 0, 0, tiled=True)  33.3 us
    all_to_all x1, blocking collectives, body(): pieces = lax.all_to_all(pieces, ('zl', 'x', 'c'), 0, 0, tiled=True)  13.8 us
    all_to_all x1, waiting for transfers between devices, body(): arrived = lax.all_to_all(crops[0], ('x', 'c'), 0, 0, tiled=True)  9.58 us
    all_to_all x1, starting transfers between devices, body(): arrived = lax.all_to_all(crops[0], ('x', 'c'), 0, 0, tiled=True)  4.44 us
    ppermute x1, starting transfers between devices, body(): lax.ppermute(right, 'ta', [(i, i + 1) for i in range(count - 1)])  3.5 us
    pallas_call x1, Pallas kernels, weigh_call(): pl.pallas_call(weigh, grid_spec=pltpu.PrefetchScalarGridSpec(num_scalar_p...  2.41 us
    ppermute x1, starting transfers between devices, body(): lax.ppermute(left, 'ta', [(i + 1, i) for i in range(count - 1)])  2.35 us
    pallas_call x1, Pallas kernels, filtered_call(): pl.pallas_call(filtered, in_specs=[pl.BlockSpec(memory_space=pltpu.SMEM),...  1.95 us
  transfers between devices with their start and end apart: 3, of which 2 were waited for; matrix products, arithmetic and copies ran while one was open for 3% of the time, Pallas kernels for 5%

profile of v7, /device:TPU:8, one launch (start us, length us, event | category | flops | bytes accessed | tf_op | source)
XLA Modules:
  0.0 81.8 jit_solution(9202427426725386064)
XLA Ops:
  0.0 0.0 copy-start.3
  0.0 0.0 copy-start.2
  0.0 0.0 copy-start.1
  0.0 0.0 copy-start
  0.0 4.4 %all-to-all-start.2 = ((bf16[32,160,128]{2,1,0:T(8,128)(2,1)}), bf16[32,160,128]{2,1,0:T(8,128)(2,1)S(1)}, u32[]{:S(2)}, u32[]{:S(2)}) async-start(bf16[32,160,128]{2,1,0:T(8,128)(2,1)} %bitcast.12), calls=%async_computation.2 | async-start | bytes 2621440 | tf_op jit(solution)/shard_map/all_to_all | solution.py:278
  4.5 0.0 copy-done.3
  4.5 0.7 fusion
  9.6 0.0 copy-done.2
  9.6 0.1 copy.10
  9.7 0.6 reshape.6.filt
  10.3 0.0 copy-done.1
  10.3 0.9 %copy.11.taps = f32[2,256,4]{2,1,0:T(8,128)} copy(f32[2,256,4]{1,2,0:T(4,128)S(1)} %copy-done.1) | data formatting | bytes 16384 | tf_op args[5]
  11.2 0.1 stack.19.meta
  11.2 2.4 %weigh.1 = (bf16[256,256]{1,0:T(8,128)(2,1)S(1)}, f32[8,128]{1,0:T(8,128)S(1)}) custom-call(s32[8]{0:T(128)S(1)} %stack.19.meta, f32[72]{0:T(128)} %reshape.6.filt, s32[2,256]{1,0:T(2,128)} %offsets.1, s32[2,256]{1,0:T(2,128)} %bands.1, f32[2,256,4]{2,1,0:T(8,128)} %copy.11.taps), custom_call_target="tpu_custom_call" | custom-call | tf_op jit(solution)/shard_map/weigh/pallas_call | solution.py:128
  13.7 9.6 %all-to-all-done.2 = bf16[32,160,128]{2,1,0:T(8,128)(2,1)S(1)} async-done(((bf16[32,160,128]{2,1,0:T(8,128)(2,1)}), bf16[32,160,128]{2,1,0:T(8,128)(2,1)S(1)}, u32[]{:S(2)}, u32[]{:S(2)}) %all-to-all-start.2) | async-done | bytes 1310752 | tf_op jit(solution)/shard_map/all_to_all | solution.py:278
  23.2 0.0 copy-done
  23.2 34.6 %conditional.2 = (f32[32,16,128]{2,1,0:T(8,128)S(1)}) conditional(s32[]{:T(128)} %convert_element_type.11, (s32[8]{0:T(128)S(1)}, bf16[8,4,160,128]{3,2,1,0:T(8,128)(2,1)S(1)}, bf16[32,128,128]{2,1,0:T(8,128)(2,1)S(1)}) %tuple.26, (s32[8]{0:T(128)S(1)}, bf16[8,4,160,128]{3,2,1,0:T(8,128)(2,1)S(1)}, bf16[32,128,128]{2,1,0:T(8,128)(2,1)S(1)}) %tuple.27), branch_computations={%region_0.1_spmd, %region_1.2_spmd} | conditional | bytes 1048584
  23.2 0.6 arrange.2
  23.8 33.3 %all_to_all.18.first.second = bf16[16,1,4,16,128]{4,3,2,1,0:T(8,128)(2,1)S(1)} all-to-all(bf16[16,1,4,16,128]{4,3,2,1,0:T(8,128)(2,1)S(1)} %arrange.2), channel_id=1, replica_groups=mesh['zh'=4,'zl'=4,'x'=4,'c'=2,'ta'=4] {'zh','zl'}, dimensions={0} | all-to-all | bytes 524288 | tf_op jit(solution)/shard_map/cond/branch_0_fun/all_to_all | solution.py:266
  57.2 0.6 products.2
  57.9 13.8 %all_to_all.20 = f16[32,16,128]{2,1,0:T(8,128)(2,1)S(1)} all-to-all(f16[32,16,128]{2,1,0:T(8,128)(2,1)S(1)} %convert_element_type.12), channel_id=1, replica_groups=mesh['zh'=4,'zl'=4,'x'=4,'c'=2,'ta'=4] {'zl','x','c'}, dimensions={0} | all-to-all | bytes 262144 | tf_op jit(solution)/shard_map/all_to_all | solution.py:288
  71.7 0.5 brink.1
  72.2 3.5 %collective-permute-start = (f32[1,256]{1,0:T(1,128)S(1)}, f32[1,256]{1,0:T(1,128)S(1)}, u32[]{:S(2)}, u32[]{:S(2)}) collective-permute-start(f32[1,256]{1,0:T(1,128)S(1)} %get-tuple-element.42), channel_id=1, source_target_pairs={{0,1},{1,2},{2,3},{4,5},{5,6},{6,7},{8,9},{9,10},{10,11},{12,13},{... | collective-permute-start | bytes 3080 | tf_op jit(solution)/shard_map/ppermute | solution.py:294
  75.7 2.4 %collective-permute-start.1 = (f32[1,256]{1,0:T(1,128)S(1)}, f32[1,256]{1,0:T(1,128)S(1)}, u32[]{:S(2)}, u32[]{:S(2)}) collective-permute-start(f32[1,256]{1,0:T(1,128)S(1)} %get-tuple-element.43), channel_id=1, source_target_pairs={{1,0},{2,1},{3,2},{5,4},{6,5},{7,6},{9,8},{10,9},{11,10},{13,12},{... | collective-permute-start | bytes 3080 | tf_op jit(solution)/shard_map/ppermute | solution.py:295
  78.0 2.0 %filtered.1.cost = f32[256,128]{1,0:T(8,128)S(1)} custom-call(f32[72]{0:T(128)} %reshape.6.filt, bf16[256,256]{1,0:T(8,128)(2,1)S(1)} %get-tuple-element.39.weights, f32[32,16,128]{2,1,0:T(8,128)S(1)} %convert_element_type.13.pieces), custom_call_target="tpu_custom_call" | custom-call | tf_op jit(solution)/shard_map/filtered/pallas_call | solution.py:229
  80.0 0.0 collective-permute-done.from_left
  80.0 1.1 %collective-permute-done.1.from_right = f32[1,256]{1,0:T(1,128)S(1)} collective-permute-done((f32[1,256]{1,0:T(1,128)S(1)}, f32[1,256]{1,0:T(1,128)S(1)}, u32[]{:S(2)}, u32[]{:S(2)}) %collective-permute-start.1) | collective-permute-done | bytes 1056 | tf_op jit(solution)/shard_map/ppermute | solution.py:295
  81.1 0.7 expected.1
  (3 shorter events, 0.1 us)
Async XLA Ops:
  0.0 4.5 %copy-start.3 = (s32[2]{0:T(128)S(1)}, s32[2]{0:T(128)}, u32[]{:S(2)}) copy-start(s32[2]{0:T(128)} %param.11) | copy-start | bytes 28
  0.0 9.6 %copy-start.2 = (f32[8,3,3]{0,2,1:T(4,128)S(1)}, f32[8,3,3]{0,2,1:T(4,128)}, u32[]{:S(2)}) copy-start(f32[8,3,3]{0,2,1:T(4,128)} %param.15) | copy-start | bytes 868
  0.0 10.3 %copy-start.1 = (f32[2,256,4]{1,2,0:T(4,128)S(1)}, f32[2,256,4]{1,2,0:T(4,128)}, u32[]{:S(2)}) copy-start(f32[2,256,4]{1,2,0:T(4,128)} %param.14) | copy-start | bytes 24580
  0.0 23.2 %copy-start = (bf16[32,128,128]{2,1,0:T(8,128)(2,1)S(1)}, bf16[32,128,128]{2,1,0:T(8,128)(2,1)}, u32[]{:S(2)}) copy-start(bf16[32,128,128]{2,1,0:T(8,128)(2,1)} %param.9) | copy-start | bytes 3145732
  0.0 23.2 %all-to-all-start.2 = ((bf16[32,160,128]{2,1,0:T(8,128)(2,1)}), bf16[32,160,128]{2,1,0:T(8,128)(2,1)S(1)}, u32[]{:S(2)}, u32[]{:S(2)}) async-start(bf16[32,160,128]{2,1,0:T(8,128)(2,1)} %bitcast.12), calls=%async_computation.2 | async-start | bytes 2621440 | tf_op jit(solution)/shard_map/all_to_all | solution.py:278
  72.2 7.8 %collective-permute-start = (f32[1,256]{1,0:T(1,128)S(1)}, f32[1,256]{1,0:T(1,128)S(1)}, u32[]{:S(2)}, u32[]{:S(2)}) collective-permute-start(f32[1,256]{1,0:T(1,128)S(1)} %get-tuple-element.42), channel_id=1, source_target_pairs={{0,1},{1,2},{2,3},{4,5},{5,6},{6,7},{8,9},{9,10},{10,11},{12,13},{... | collective-permute-start | bytes 3080 | tf_op jit(solution)/shard_map/ppermute | solution.py:294
  75.7 5.5 %collective-permute-start.1 = (f32[1,256]{1,0:T(1,128)S(1)}, f32[1,256]{1,0:T(1,128)S(1)}, u32[]{:S(2)}, u32[]{:S(2)}) collective-permute-start(f32[1,256]{1,0:T(1,128)S(1)} %get-tuple-element.43), channel_id=1, source_target_pairs={{1,0},{2,1},{3,2},{5,4},{6,5},{7,6},{9,8},{10,9},{11,10},{13,12},{... | collective-permute-start | bytes 3080 | tf_op jit(solution)/shard_map/ppermute | solution.py:295

commit v8 on v7

--- a/solution.py
+++ b/solution.py
@@ -99,7 +99,8 @@
         for group in range(G):
             rows = jnp.where((lag == i) & (slot == group), filt[group * 9 + i * 3], rows)
             rows = jnp.where((lag == i) & (slot == G + group), filt[group * 9 + i * 3 + 2], rows)
-    lines[...] = rows
+    even = jnp.where(jnp.bitwise_and(meta[8], 1) == 0, 1.0, 0.0)
+    lines[...] = jnp.where(lag == 3, even, rows)
     sub = lax.broadcasted_iota(jnp.int32, (128, D), 0)
     packed = jnp.zeros((128, D), jnp.float32)
     for view in range(2):
@@ -165,8 +166,11 @@
         sums[i, D + 8 : D + 16, :] = zero
         sums[i, 8 : D + 8, :] = part * line
     total = (sums[0, 7 : D + 7, :] + sums[1, 8 : D + 8, :] + sums[2, 9 : D + 9, :]).T
-    right[...] = jnp.sum(total[0:G], axis=0, keepdims=True)
-    left[...] = jnp.sum(total[G : 2 * G], axis=0, keepdims=True)
+    onward = jnp.sum(total[0:G], axis=0, keepdims=True)
+    back = jnp.sum(total[G : 2 * G], axis=0, keepdims=True)
+    even = jnp.concatenate([lines[3:4, :], lines[3:4, :]], axis=1) > 0.5
+    right[...] = jnp.where(even, onward, back)
+    left[...] = jnp.where(even, back, onward)
 
 
 def brink_call(lines, weights, pieces):
@@ -243,9 +247,12 @@
     )(filt, weights, pieces)
 
 
-def expected(cost, from_left, from_right, out):
+def expected(cost, lines, pair, cross, out):
     sub = lax.broadcasted_iota(jnp.int32, (128, D), 0)
-    edges = jnp.where(sub == 0, from_left[...], jnp.where(sub == 127, from_right[...], 0.0)).T
+    even = jnp.concatenate([lines[3:4, :], lines[3:4, :]], axis=1) > 0.5
+    from_left = jnp.where(even, cross[...], pair[...])
+    from_right = jnp.where(even, pair[...], cross[...])
+    edges = jnp.where(sub == 0, from_left, jnp.where(sub == 127, from_right, 0.0)).T
     whole = cost[...] + edges
     top = jnp.max(whole, axis=0, keepdims=True)
     grown = jnp.exp(whole - top)
@@ -253,12 +260,12 @@
     out[...] = jnp.sum(grown * heights, axis=0, keepdims=True) / jnp.sum(grown, axis=0, keepdims=True)
 
 
-def expected_call(cost, from_left, from_right):
+def expected_call(cost, lines, pair, cross):
     return pl.pallas_call(
         expected,
         out_shape=jax.ShapeDtypeStruct((1, 128), jnp.float32),
         name="expected",
-    )(cost, from_left, from_right)
+    )(cost, lines, pair, cross)
 
 
 def spread(meta, arrived, ref_feats, picks):
@@ -274,7 +281,7 @@
     near = owner % G
     far = owner // G
     mine = jnp.where(far[1] == block * ZL + phase, near[1], near[0])
-    meta = jnp.stack([near[0], near[1], far[0], far[1], block, phase, group, mine]).astype(jnp.int32)
+    meta = jnp.stack([near[0], near[1], far[0], far[1], block, phase, group, mine, lax.axis_index("ta")]).astype(jnp.int32)
     arrived = lax.all_to_all(crops[0], ("x", "c"), 0, 0, tiled=True)
     filt = filt.reshape(G * 9)
     weights, lines = weigh_call(meta, filt, offsets, bands, taps)
@@ -291,10 +298,10 @@
     pieces = near_core(pieces)
     right, left = brink_call(near_core(lines), weights, pieces)
     count = lax.axis_size("ta")
-    from_left = lax.ppermute(right, "ta", [(i, i + 1) for i in range(count - 1)])
-    from_right = lax.ppermute(left, "ta", [(i + 1, i) for i in range(count - 1)])
+    pair = lax.ppermute(right, "ta", [(i, i ^ 1) for i in range(count) if i ^ 1 < count])
+    cross = lax.ppermute(left, "ta", [p for i in range(1, count - 1, 2) for p in ((i, i + 1), (i + 1, i))])
     cost = filtered_call(filt, weights, pieces)
-    return expected_call(near_core(cost), near_core(from_left), near_core(from_right))
+    return expected_call(near_core(cost), near_core(lines), near_core(pair), near_core(cross))
 
 
 def solution(mesh):

time: 82.2 us -> 81.9 us (level)
  waiting for transfers between devices: 10.7 us -> 9.59 us
    ppermute x2, waiting for transfers between devices: 1.14 us -> 0.01 us  [the longest x1 0.01 us: body(): lax.ppermute(right, 'ta', [(i, i ^ 1) for i in range(count) if i ^ 1 < co...]
    ppermute x2, starting transfers between devices: 5.85 us -> 6.69 us  [the longest x1 4.32 us: body(): lax.ppermute(left, 'ta', [p for i in range(1, count - 1, 2) for p in ((i,...]
  transfers between devices with their start and end apart: 3 -> 3, of which waited for: 2 -> 1; matrix products, arithmetic and copies ran while one was open for 3% -> 3% of each run, Pallas kernels for 5% -> 5%
where the time goes in v8:
time: 81.9 us; the launch traced here: 81.5 us
  blocking collectives  47.1 us (58%)
  starting transfers between devices  11.1 us (14%)
  waiting for transfers between devices  9.59 us (12%)
  Pallas kernels  6.75 us (8%)
  between operations  4.53 us (6%)
  local copies, waits for them, and re-layouts  2.33 us (3%)
    all_to_all x1, blocking collectives, spread(): windows = lax.all_to_all(windows, ('zh', 'zl'), 0, 0, tiled=True)  33.3 us
    all_to_all x1, blocking collectives, body(): pieces = lax.all_to_all(pieces, ('zl', 'x', 'c'), 0, 0, tiled=True)  13.8 us
    all_to_all x1, waiting for transfers between devices, body(): arrived = lax.all_to_all(crops[0], ('x', 'c'), 0, 0, tiled=True)  9.58 us
    all_to_all x1, starting transfers between devices, body(): arrived = lax.all_to_all(crops[0], ('x', 'c'), 0, 0, tiled=True)  4.44 us
    ppermute x1, starting transfers between devices, body(): lax.ppermute(left, 'ta', [p for i in range(1, count - 1, 2) for p in ((i,...  4.32 us
    pallas_call x1, Pallas kernels, weigh_call(): pl.pallas_call(weigh, grid_spec=pltpu.PrefetchScalarGridSpec(num_scalar_p...  2.41 us
    ppermute x1, starting transfers between devices, body(): lax.ppermute(right, 'ta', [(i, i ^ 1) for i in range(count) if i ^ 1 < co...  2.37 us
    pallas_call x1, Pallas kernels, filtered_call(): pl.pallas_call(filtered, in_specs=[pl.BlockSpec(memory_space=pltpu.SMEM),...  1.95 us
  transfers between devices with their start and end apart: 3, of which 1 were waited for; matrix products, arithmetic and copies ran while one was open for 3% of the time, Pallas kernels for 5%

profile of v8, /device:TPU:8, one launch (start us, length us, event | category | flops | bytes accessed | tf_op | source)
XLA Modules:
  0.0 81.5 jit_solution(14036647083262558408)
XLA Ops:
  0.0 0.0 copy-start.3
  0.0 0.0 copy-start.2
  0.0 0.0 copy-start.1
  0.0 0.0 copy-start
  0.0 4.4 %all-to-all-start.2 = ((bf16[32,160,128]{2,1,0:T(8,128)(2,1)}), bf16[32,160,128]{2,1,0:T(8,128)(2,1)S(1)}, u32[]{:S(2)}, u32[]{:S(2)}) async-start(bf16[32,160,128]{2,1,0:T(8,128)(2,1)} %bitcast.13), calls=%async_computation.2 | async-start | bytes 2621440 | tf_op jit(solution)/shard_map/all_to_all | solution.py:285
  4.5 0.0 copy-done.3
  4.5 0.7 fusion
  9.6 0.0 copy-done.2
  9.6 0.1 copy.10
  9.7 0.6 reshape.6.filt
  10.3 0.0 copy-done.1
  10.3 0.9 %copy.11.taps = f32[2,256,4]{2,1,0:T(8,128)} copy(f32[2,256,4]{1,2,0:T(4,128)S(1)} %copy-done.1) | data formatting | bytes 16384 | tf_op args[5]
  11.2 0.1 stack.23.meta
  11.2 2.4 %weigh.1 = (bf16[256,256]{1,0:T(8,128)(2,1)S(1)}, f32[8,128]{1,0:T(8,128)S(1)}) custom-call(s32[9]{0:T(128)S(1)} %stack.23.meta, f32[72]{0:T(128)} %reshape.6.filt, s32[2,256]{1,0:T(2,128)} %offsets.1, s32[2,256]{1,0:T(2,128)} %bands.1, f32[2,256,4]{2,1,0:T(8,128)} %copy.11.taps), custom_call_target="tpu_custom_call" | custom-call | tf_op jit(solution)/shard_map/weigh/pallas_call | solution.py:129
  13.7 9.6 %all-to-all-done.2 = bf16[32,160,128]{2,1,0:T(8,128)(2,1)S(1)} async-done(((bf16[32,160,128]{2,1,0:T(8,128)(2,1)}), bf16[32,160,128]{2,1,0:T(8,128)(2,1)S(1)}, u32[]{:S(2)}, u32[]{:S(2)}) %all-to-all-start.2) | async-done | bytes 1310752 | tf_op jit(solution)/shard_map/all_to_all | solution.py:285
  23.2 0.0 copy-done
  23.2 34.6 %conditional.2 = (f32[32,16,128]{2,1,0:T(8,128)S(1)}) conditional(s32[]{:T(128)} %convert_element_type.11, (s32[9]{0:T(128)S(1)}, bf16[8,4,160,128]{3,2,1,0:T(8,128)(2,1)S(1)}, bf16[32,128,128]{2,1,0:T(8,128)(2,1)S(1)}) %tuple.26, (s32[9]{0:T(128)S(1)}, bf16[8,4,160,128]{3,2,1,0:T(8,128)(2,1)S(1)}, bf16[32,128,128]{2,1,0:T(8,128)(2,1)S(1)}) %tuple.27), branch_computations={%region_0.1_spmd, %region_1.2_spmd} | conditional | bytes 1048584
  23.2 0.6 arrange.2
  23.8 33.3 %all_to_all.18.first.second = bf16[16,1,4,16,128]{4,3,2,1,0:T(8,128)(2,1)S(1)} all-to-all(bf16[16,1,4,16,128]{4,3,2,1,0:T(8,128)(2,1)S(1)} %arrange.2), channel_id=1, replica_groups=mesh['zh'=4,'zl'=4,'x'=4,'c'=2,'ta'=4] {'zh','zl'}, dimensions={0} | all-to-all | bytes 524288 | tf_op jit(solution)/shard_map/cond/branch_0_fun/all_to_all | solution.py:273
  57.2 0.6 products.2
  57.9 13.8 %all_to_all.20 = f16[32,16,128]{2,1,0:T(8,128)(2,1)S(1)} all-to-all(f16[32,16,128]{2,1,0:T(8,128)(2,1)S(1)} %convert_element_type.12), channel_id=1, replica_groups=mesh['zh'=4,'zl'=4,'x'=4,'c'=2,'ta'=4] {'zl','x','c'}, dimensions={0} | all-to-all | bytes 262144 | tf_op jit(solution)/shard_map/all_to_all | solution.py:295
  71.7 0.5 brink.1
  72.2 2.4 %collective-permute-start = (f32[1,256]{1,0:T(1,128)S(1)}, f32[1,256]{1,0:T(1,128)S(1)}, u32[]{:S(2)}, u32[]{:S(2)}) collective-permute-start(f32[1,256]{1,0:T(1,128)S(1)} %get-tuple-element.42), channel_id=1, source_target_pairs={{0,1},{1,0},{2,3},{3,2},{4,5},{5,4},{6,7},{7,6},{8,9},{9,8},{10,11... | collective-permute-start | bytes 3080 | tf_op jit(solution)/shard_map/ppermute | solution.py:301
  74.5 4.3 %collective-permute-start.1 = (f32[1,256]{1,0:T(1,128)S(1)}, f32[1,256]{1,0:T(1,128)S(1)}, u32[]{:S(2)}, u32[]{:S(2)}) collective-permute-start(f32[1,256]{1,0:T(1,128)S(1)} %get-tuple-element.43), channel_id=1, source_target_pairs={{1,2},{2,1},{5,6},{6,5},{9,10},{10,9},{13,14},{14,13},{17,18},{18,... | collective-permute-start | bytes 3080 | tf_op jit(solution)/shard_map/ppermute | solution.py:302
  78.9 2.0 %filtered.1.cost = f32[256,128]{1,0:T(8,128)S(1)} custom-call(f32[72]{0:T(128)} %reshape.6.filt, bf16[256,256]{1,0:T(8,128)(2,1)S(1)} %get-tuple-element.39.weights, f32[32,16,128]{2,1,0:T(8,128)S(1)} %convert_element_type.13.pieces), custom_call_target="tpu_custom_call" | custom-call | tf_op jit(solution)/shard_map/filtered/pallas_call | solution.py:233
  80.8 0.0 collective-permute-done.pair
  80.8 0.0 collective-permute-done.1.cross
  80.8 0.7 expected.1
  (3 shorter events, 0.1 us)
Async XLA Ops:
  0.0 4.5 %copy-start.3 = (s32[2]{0:T(128)S(1)}, s32[2]{0:T(128)}, u32[]{:S(2)}) copy-start(s32[2]{0:T(128)} %param.11) | copy-start | bytes 28
  0.0 9.6 %copy-start.2 = (f32[8,3,3]{0,2,1:T(4,128)S(1)}, f32[8,3,3]{0,2,1:T(4,128)}, u32[]{:S(2)}) copy-start(f32[8,3,3]{0,2,1:T(4,128)} %param.15) | copy-start | bytes 868
  0.0 10.3 %copy-start.1 = (f32[2,256,4]{1,2,0:T(4,128)S(1)}, f32[2,256,4]{1,2,0:T(4,128)}, u32[]{:S(2)}) copy-start(f32[2,256,4]{1,2,0:T(4,128)} %param.14) | copy-start | bytes 24580
  0.0 23.2 %copy-start = (bf16[32,128,128]{2,1,0:T(8,128)(2,1)S(1)}, bf16[32,128,128]{2,1,0:T(8,128)(2,1)}, u32[]{:S(2)}) copy-start(bf16[32,128,128]{2,1,0:T(8,128)(2,1)} %param.9) | copy-start | bytes 3145732
  0.0 23.2 %all-to-all-start.2 = ((bf16[32,160,128]{2,1,0:T(8,128)(2,1)}), bf16[32,160,128]{2,1,0:T(8,128)(2,1)S(1)}, u32[]{:S(2)}, u32[]{:S(2)}) async-start(bf16[32,160,128]{2,1,0:T(8,128)(2,1)} %bitcast.13), calls=%async_computation.2 | async-start | bytes 2621440 | tf_op jit(solution)/shard_map/all_to_all | solution.py:285
  72.2 8.7 %collective-permute-start = (f32[1,256]{1,0:T(1,128)S(1)}, f32[1,256]{1,0:T(1,128)S(1)}, u32[]{:S(2)}, u32[]{:S(2)}) collective-permute-start(f32[1,256]{1,0:T(1,128)S(1)} %get-tuple-element.42), channel_id=1, source_target_pairs={{0,1},{1,0},{2,3},{3,2},{4,5},{5,4},{6,7},{7,6},{8,9},{9,8},{10,11... | collective-permute-start | bytes 3080 | tf_op jit(solution)/shard_map/ppermute | solution.py:301
  74.5 6.3 %collective-permute-start.1 = (f32[1,256]{1,0:T(1,128)S(1)}, f32[1,256]{1,0:T(1,128)S(1)}, u32[]{:S(2)}, u32[]{:S(2)}) collective-permute-start(f32[1,256]{1,0:T(1,128)S(1)} %get-tuple-element.43), channel_id=1, source_target_pairs={{1,2},{2,1},{5,6},{6,5},{9,10},{10,9},{13,14},{14,13},{17,18},{18,... | collective-permute-start | bytes 3080 | tf_op jit(solution)/shard_map/ppermute | solution.py:302
